TPU v7x, 32 devices: a whole 2x2x4 slice. The times are simulated.
32 devices in a mesh: sec: 2 (over core), grp: 4 (over y, x), dev: 4 (over z).
Axes of the slice: x: 2, y: 2, z: 4, core: 2. Of those that a mesh axis runs over, the one named last changes fastest.
Arguments:
- current: float32 [32, 196608], P(None, ('sec', 'grp', 'dev')), may hold values from -6 to 6
- prior: float32 [8, 32, 196608], P(None, None, ('sec', 'grp', 'dev')), as said below
- block_values: float32 [1024, 6, 9216], P(('grp', 'dev')), may hold values from -0.25 to 0.25
- block_cols: int32 [1024, 6], P(('grp', 'dev')), may hold values from 0 to 63
- face_match: int32 [16, 4, 1536], P(('grp', 'dev')), may hold values from 0 to 1535, each once within a row
- face_weight: float32 [16, 4, 1536], P(('grp', 'dev')), may hold values from -3 to 3
- fluid_diag: float32 [98304], P(('grp', 'dev')), may hold values from 2 to 4
- wet_source: int32 [49152], P(('grp', 'dev')), may hold values from 0 to 6143
- wet_dest: int32 [49152, 1], P(('grp', 'dev')), may hold values from 0 to 15; in each aligned block of 3072 rows (0 to 3071, 3072 to 6143, ...) at most 392 rows name the same one
- wet_target: int32 [49152], P(('grp', 'dev')), may hold values from 0 to 6143
- wet_weight: float32 [49152], P(('grp', 'dev')), may hold values from -5 to 5
Outputs:
- next_block: float32 [32, 196608], P(None, ('sec', 'grp', 'dev'))
- coeffs: float32 [8, 32, 32], replicated
- rfac: float32 [32, 32], replicated
Inputs may be any that keep to these rules, and one draw needn't show every extreme that they name: `block_cols`: block columns index blocks within the same subdomain. `face_match`: each subdomain's matching of one round is a permutation of its face. `prior`: each earlier block's columns have about unit length. `wet_dest`: among one structure subdomain's couplings, at most 392 name the same fluid subdomain, and some subdomain has exactly 392 for one.
All inputs are finite; a program needn't handle non-finite values.
Results may differ from a plain program's by a relative error of at most 0.00008.
Values sent between devices are 32-bit elements; how exact they have to be, the bound alone decides.
A program may use at most 128 MiB of HBM per device.

v0:
```python
import functools

import jax
import jax.numpy as jnp
from jax import lax
from jax.experimental import pallas as pl
from jax.experimental.pallas import tpu as pltpu
from jax.sharding import PartitionSpec as P

BS = 96
NB = 6
ROUNDS = 4
LANES = 128
META = 8
F32 = jnp.float32
BF16 = jnp.bfloat16
NT = (((1,), (1,)), ((), ()))
ALL = ("sec", "grp", "dev")


def split2(x):
    hi = x.astype(BF16)
    return hi, (x - hi.astype(F32)).astype(BF16)


def nt(a, b):
    return lax.dot_general(a, b, NT, preferred_element_type=F32)


def lane_gather(x, low):
    return jnp.take_along_axis(x, low, axis=1)


def wet_kernel(
    subdomains, per, x_ref, xs_ref, diag_ref, edge_ref, src_ref, dest_ref, tgt_ref, w_ref, out_ref,
    meta_ref, pack_ref, got_ref, lhs_ref, acc_ref, sems,
):
    @pl.when(lax.axis_index("sec") == 1)
    def _():
        wet_body(
            subdomains, per, x_ref, xs_ref, diag_ref, edge_ref, src_ref, dest_ref, tgt_ref, w_ref,
            out_ref, meta_ref, pack_ref, got_ref, lhs_ref, acc_ref, sems,
        )


def wet_body(
    subdomains, per, own_ref, x_ref, diag_ref, edge_ref, src_ref, dest_ref, tgt_ref, w_ref, image_ref,
    meta_ref, pack_ref, got_ref, lhs_ref, acc_ref, sems,
):
    mine = lax.axis_index("grp") * lax.axis_size("dev") + lax.axis_index("dev")
    barrier = pltpu.get_barrier_semaphore()

    def greet(i, carry):
        other = subdomains + lax.rem(mine + i, subdomains)
        pl.semaphore_signal(barrier, inc=1, device_id=place(other), device_id_type=MESH)
        return carry

    lax.fori_loop(1, subdomains, greet, 0)
    width, rows = x_ref.shape
    blocks = src_ref.shape[0]
    slabs = subdomains * per
    dest = dest_ref[...]
    lane = lax.broadcasted_iota(jnp.int32, (LANES, LANES), 1)
    sub = lax.broadcasted_iota(jnp.int32, (LANES, LANES), 0)
    tri = jnp.where(sub < lane, 1.0, 0.0).astype(BF16)
    ones = jnp.ones((LANES, LANES), BF16)
    low_tri = jnp.where(
        lax.broadcasted_iota(jnp.int32, (blocks, blocks), 1)
        < lax.broadcasted_iota(jnp.int32, (blocks, blocks), 0),
        1.0,
        0.0,
    ).astype(BF16)

    def count(q, rank):
        mine = dest == q
        oh = jnp.where(mine, 1.0, 0.0).astype(BF16)
        within = jnp.dot(oh, tri, preferred_element_type=F32)
        totals = jnp.dot(oh, ones, preferred_element_type=F32).astype(BF16)
        offset = jnp.dot(low_tri, totals, preferred_element_type=F32)
        return jnp.where(mine, within + offset, rank)

    rank = lax.fori_loop(0, subdomains, count, jnp.zeros(dest.shape, F32)).astype(jnp.int32)
    slab = dest * per + rank // LANES
    spot = rank % LANES
    src = src_ref[...]
    tgt = tgt_ref[...]
    w = w_ref[...]
    w0 = w.astype(BF16).astype(F32)
    w1 = (w - w0).astype(BF16).astype(F32)
    w2 = w - w0 - w1
    fields = [src // LANES, src % LANES, tgt // LANES, tgt % LANES]
    fields = [f.astype(F32) for f in fields] + [w0, w1, w2]
    acc = jnp.zeros((len(fields) * slabs, LANES), F32)
    slab_row = lax.broadcasted_iota(jnp.int32, (slabs, LANES), 0)
    for i in range(blocks):
        hit = slab_row == slab[i : i + 1, :]
        lhs = jnp.concatenate([jnp.where(hit, f[i : i + 1, :], 0.0) for f in fields], axis=0)
        oh = jnp.where(sub == spot[i : i + 1, :], 1.0, 0.0)
        acc = acc + nt(lhs.astype(BF16), oh.astype(BF16))
    parts = [acc[f * slabs : (f + 1) * slabs] for f in range(len(fields))]
    meta_ref[0] = parts[0]
    meta_ref[1] = parts[1]
    meta_ref[2] = parts[2] * LANES + parts[3]
    meta_ref[3] = parts[4] + parts[5] + parts[6]

    def gather(a, ref, to):
        row = pl.ds(a, 1)
        high = jnp.broadcast_to(meta_ref[0, row, :].astype(jnp.int32), (width, LANES))
        low = jnp.broadcast_to(meta_ref[1, row, :].astype(jnp.int32), (width, LANES))
        got = jnp.zeros((width, LANES), F32)
        for h in range(rows // LANES):
            piece = lane_gather(x_ref[:, h * LANES : (h + 1) * LANES], low)
            got = jnp.where(high == h, piece, got)
        ref[to, :width, :] = got * meta_ref[3, row, :]
        ref[to, width:, :] = jnp.broadcast_to(meta_ref[2, row, :], (META, LANES))

    def copy(to, at):
        return remote(
            pack_ref.at[pl.ds(to * per, per)], got_ref.at[pl.ds(at * per, per)], sems.at[0, to],
            sems.at[1, at], place(subdomains + to),
        )

    pl.semaphore_wait(barrier, subdomains - 1)

    def send(s, carry):
        q = lax.rem(mine + s, subdomains)

        def one(p, inner):
            gather(q * per + p, pack_ref, q * per + p)
            return inner

        lax.fori_loop(0, per, one, 0)
        copy(q, mine).start()
        return carry

    lax.fori_loop(1, subdomains, send, 0)

    def keep(p, inner):
        gather(mine * per + p, got_ref, mine * per + p)
        return inner

    lax.fori_loop(0, per, keep, 0)
    wide = 2 * LANES
    highs = rows // wide
    acc_ref[...] = jnp.zeros_like(acc_ref)

    def add(q):
        ohs = []
        for s in range(per):
            a = q * per + s
            target = got_ref[a, width : width + 1, :].astype(jnp.int32)
            vals = got_ref[a, :width, :]
            hi = vals.astype(BF16).astype(F32)
            lo = vals - hi
            high = jnp.broadcast_to(target // wide, (width, LANES))
            low = target % wide
            at = s * wide
            for h in range(highs):
                hit = high == h
                band = slice(h * width, (h + 1) * width)
                lhs_ref[band, at : at + LANES] = jnp.where(hit, hi, 0.0).astype(BF16)
                lhs_ref[band, at + LANES : at + wide] = jnp.where(hit, lo, 0.0).astype(BF16)
            oh = jnp.where(
                lax.broadcasted_iota(jnp.int32, (wide, LANES), 0) == low, 1.0, 0.0
            ).astype(BF16)
            ohs += [oh, oh]
        acc_ref[...] += nt(lhs_ref[...], jnp.concatenate(ohs, axis=1))

    add(mine)

    def take(s, carry):
        q = lax.rem(mine + subdomains - s, subdomains)
        copy(q, q).wait_recv()
        add(q)
        return carry

    lax.fori_loop(1, subdomains, take, 0)

    def drain(s, carry):
        copy(lax.rem(mine + s, subdomains), mine).wait_send()
        return carry

    lax.fori_loop(1, subdomains, drain, 0)
    edges = [
        jnp.where(mine == 0, 0.0, edge_ref[0]),
        jnp.where(mine == subdomains - 1, 0.0, edge_ref[1]),
    ]
    lane = lax.broadcasted_iota(jnp.int32, (width, LANES), 1)
    pieces = rows // LANES
    for t in range(pieces):
        own = own_ref[:, t * LANES : (t + 1) * LANES]
        prev = edges[0] if t == 0 else own_ref[:, (t - 1) * LANES : t * LANES]
        nxt = edges[1] if t == pieces - 1 else own_ref[:, (t + 1) * LANES : (t + 2) * LANES]
        before = jnp.where(lane == 0, pltpu.roll(prev, 1, 1), pltpu.roll(own, 1, 1))
        after = jnp.where(
            lane == LANES - 1, pltpu.roll(nxt, LANES - 1, 1), pltpu.roll(own, LANES - 1, 1)
        )
        h, side = t // 2, t % 2
        added = acc_ref[h * width : (h + 1) * width, side * LANES : (side + 1) * LANES]
        d = diag_ref[:, t * LANES : (t + 1) * LANES]
        image_ref[:, t * LANES : (t + 1) * LANES] = d * own - before - after + added


def face_kernel(y_ref, faces_ref, match_ref, weight_ref, out_ref):
    width = y_ref.shape[0]
    rounds, face = match_ref.shape
    pieces = face // LANES
    for m in range(rounds):
        for o in range(pieces):
            index = match_ref[m : m + 1, o * LANES : (o + 1) * LANES]
            high = jnp.broadcast_to(index // LANES, (width, LANES))
            low = jnp.broadcast_to(index % LANES, (width, LANES))
            got = jnp.zeros((width, LANES), F32)
            for h in range(pieces):
                piece = lane_gather(faces_ref[m, :, h * LANES : (h + 1) * LANES], low)
                got = jnp.where(high == h, piece, got)
            at = m * face + o * LANES
            w = weight_ref[m : m + 1, o * LANES : (o + 1) * LANES]
            out_ref[:, at : at + LANES] = y_ref[:, at : at + LANES] + w * got
    done = rounds * face
    if done < y_ref.shape[1]:
        out_ref[:, done:] = y_ref[:, done:]


MESH = pl.DeviceIdType.MESH


def place(index):
    dev = lax.axis_size("dev")
    grp = lax.axis_size("grp")
    return (index // (grp * dev), index // dev % grp, index % dev)


def own_index():
    grp, dev = lax.axis_size("grp"), lax.axis_size("dev")
    return (lax.axis_index("sec") * grp + lax.axis_index("grp")) * dev + lax.axis_index("dev")


def everyone(body):
    counts = [lax.axis_size(axis) for axis in ALL]
    turns = []
    for axis, count in zip(ALL, counts):
        at = lax.axis_index(axis)
        ring = [at]
        for _ in range(1, count):
            following = ring[-1] + 1
            ring.append(jnp.where(following == count, 0, following))
        turns.append(ring)
    for i in range(counts[0]):
        for j in range(counts[1]):
            for k in range(counts[2]):
                if i or j or k:
                    where = (turns[0][i], turns[1][j], turns[2][k])
                    body((where[0] * counts[1] + where[1]) * counts[2] + where[2], where)


def announce():
    barrier = pltpu.get_barrier_semaphore()
    everyone(
        lambda d, where: pl.semaphore_signal(
            barrier, inc=1, device_id=where, device_id_type=MESH
        )
    )
    return barrier


def stream(prior_ref, held, sems, chunk):
    def copy(i):
        at = pl.ds(pl.multiple_of(i * chunk, chunk), chunk)
        return pltpu.make_async_copy(prior_ref.at[:, at], held.at[:, at], sems.at[i])

    return copy


def remote(src, dst, send, recv, device):
    return pltpu.make_async_remote_copy(
        src_ref=src, dst_ref=dst, send_sem=send, recv_sem=recv, device_id=device,
        device_id_type=MESH,
    )


class Summing:
    def __init__(self, me, n, stage, slots, total, sems):
        self.me, self.n = me, n
        self.stage, self.slots, self.total, self.sems = stage, slots, total, sems

    def scatter(self):
        everyone(
            lambda d, where: remote(
                self.stage.at[d], self.slots.at[self.me], self.sems.at[0], self.sems.at[1], where
            ).start()
        )

    def bulk(self, source, target, first):
        rest = pl.ds(0, self.n - 1)
        other = (1 - lax.axis_index("sec"), lax.axis_index("grp"), lax.axis_index("dev"))
        return remote(
            source.at[rest], target.at[rest], self.sems.at[first], self.sems.at[first + 1], other
        )

    def gather(self):
        me = self.me
        self.bulk(self.stage, self.slots, 0).wait_recv()
        self.slots[me] = self.stage[me]
        self.total[me] = jnp.sum(self.slots[...], axis=0)
        everyone(
            lambda d, where: remote(
                self.total.at[me], self.total.at[me], self.sems.at[2], self.sems.at[3], where
            ).start()
        )

    def finish(self):
        self.bulk(self.total, self.total, 2).wait_recv()
        self.bulk(self.stage, self.slots, 0).wait_send()
        self.bulk(self.total, self.total, 2).wait_send()


def exchange_kernel(
    subdomains, face, x_ref, prior_ref, cross_ref, faces_ref, edge_ref, xs_ref,
    stage, slots, total, sems, face_sems, edge_sems, twin_sems, held, held_sems,
):
    n = 2 * subdomains
    me = own_index()
    sec, g, d = lax.axis_index("sec"), lax.axis_index("grp"), lax.axis_index("dev")
    mine = lax.rem(me, subdomains)
    rows = x_ref.shape[1]
    partners = [
        (0, g, d + 1 - 2 * lax.rem(d, 2)),
        (0, g, d + 2 - 4 * lax.rem(d // 2, 2)),
        (0, g + 1 - 2 * lax.rem(g, 2), d),
        (0, g + 2 - 4 * lax.rem(g // 2, 2), d),
    ]

    def face_copy(m):
        return remote(
            x_ref.at[:, pl.ds(m * face, face)], faces_ref.at[m], face_sems.at[0, m],
            face_sems.at[1, m], partners[m],
        )

    def edge_copy(side):
        to = subdomains + lax.rem(mine + (1 if side == 0 else subdomains - 1), subdomains)
        at = rows - LANES if side == 0 else 0
        return remote(
            x_ref.at[:, pl.ds(at, LANES)], edge_ref.at[side], edge_sems.at[0, side],
            edge_sems.at[1, side], place(to),
        )

    def twin_copy():
        return remote(x_ref, xs_ref, twin_sems.at[0], twin_sems.at[1], (1, g, d))

    chunk = held.shape[1] // held_sems.shape[0]
    incoming = stream(prior_ref, held, held_sems, chunk)
    for i in range(rows // chunk):
        incoming(i).start()
    pl.semaphore_wait(announce(), n - 1)

    @pl.when(sec == 0)
    def _():
        twin_copy().start()
        for m in range(ROUNDS):
            face_copy(m).start()

    @pl.when(sec == 1)
    def _():
        edge_copy(0).start()
        edge_copy(1).start()

    basis = prior_ref.shape[0]

    def product(i, carry):
        same, mixed = carry
        incoming(i).wait()
        hi, lo = split2(held[:, pl.ds(pl.multiple_of(i * chunk, chunk), chunk)])
        return same + nt(hi, hi), mixed + nt(hi, lo)

    zero = jnp.zeros((basis, basis), F32)
    same, mixed = lax.fori_loop(0, rows // chunk, product, (zero, zero))
    part = same + mixed + mixed.T
    piece = basis // n
    stage[...] = part.reshape(n, piece, basis)
    summing = Summing(me, n, stage, slots, total, sems)
    summing.scatter()
    summing.gather()
    summing.finish()
    cross_ref[...] = total[...].reshape(basis, basis)

    @pl.when(sec == 0)
    def _():
        for m in range(ROUNDS):
            face_copy(m).wait()
        twin_copy().wait_send()

    @pl.when(sec == 1)
    def _():
        edge_copy(0).wait()
        edge_copy(1).wait()
        twin_copy().wait_recv()


def finish_kernel(
    subdomains, total_rows, image_ref, prior_ref, cross_ref, next_ref, coef_ref, fac_ref,
    high_ref, low_ref, stage, slots, total, sems, held, held_sems,
):
    n = 2 * subdomains
    me = own_index()
    width, rows = image_ref.shape
    basis = prior_ref.shape[0]
    chunk = held.shape[1] // held_sems.shape[0]
    incoming = stream(prior_ref, held, held_sems, chunk)
    for i in range(rows // chunk):
        incoming(i).start()
    barrier = announce()

    def product(i, carry):
        head, square = carry
        at = pl.ds(pl.multiple_of(i * chunk, chunk), chunk)
        incoming(i).wait()
        hi, lo = split2(held[:, at])
        high_ref[:, at] = hi
        low_ref[:, at] = lo
        ih, il = split2(image_ref[:, at])
        both = nt(jnp.concatenate([ih, il], axis=0), hi)
        head = head + both[:width] + both[width:] + nt(ih, lo)
        mixed = nt(ih, il)
        square = square + nt(ih, ih) + mixed + mixed.T
        return head, square

    head, square = lax.fori_loop(
        0, rows // chunk, product,
        (jnp.zeros((width, basis), F32), jnp.zeros((width, width), F32)),
    )
    part = jnp.concatenate(
        [head, square, jnp.zeros((width, -(basis + width) % LANES), F32)], axis=1
    )
    cuts = n // width
    span = part.shape[1] // cuts
    for i in range(n):
        row, cut = i // cuts, i % cuts
        stage[i] = part[row : row + 1, cut * span : (cut + 1) * span]
    pl.semaphore_wait(barrier, n - 1)
    summing = Summing(me, n, stage, slots, total, sems)
    summing.scatter()
    summing.gather()
    summing.finish()
    lines = [
        jnp.concatenate([total[r * cuts + c] for c in range(cuts)], axis=1) if cuts > 1 else total[r]
        for r in range(width)
    ]
    summed = jnp.concatenate(lines, axis=0)
    first = summed[:, :basis]
    square = summed[:, basis : basis + width]
    cross = cross_ref[...]
    highest = lax.Precision.HIGHEST

    def dot(a, b):
        return jnp.dot(a, b, precision=highest, preferred_element_type=F32)

    def dot_nt(a, b):
        return lax.dot_general(a, b, NT, precision=highest, preferred_element_type=F32)

    coef = 2.0 * first - dot(first, cross)
    gram = (
        square - dot_nt(coef, first) - dot_nt(first, coef) + dot_nt(dot(coef, cross), coef)
    ) * (1.0 / total_rows)
    coef_ref[...] = coef.T
    sub = lax.broadcasted_iota(jnp.int32, (width, 2 * width), 0)
    lane = lax.broadcasted_iota(jnp.int32, (width, 2 * width), 1)
    eye = jnp.where(sub + width == lane, 1.0, 0.0)
    work = jnp.concatenate([gram, jnp.zeros((width, width), F32)], axis=1) + eye
    for j in range(width):
        root = jnp.sqrt(work[j : j + 1, j : j + 1])
        row = work[j : j + 1, :] / root
        column = work[:, j : j + 1] / root
        work = jnp.where(sub == j, row, jnp.where(sub > j, work - column * row, work))
    fac_ref[...] = jnp.where(sub <= lane, work, 0.0)[:, :width]
    inverse = work[:, width:]
    mix = -dot(inverse, coef)
    vh, vl = split2(inverse)
    mh, ml = split2(mix)
    vs = jnp.concatenate([vh, vl], axis=0)
    ms = jnp.concatenate([mh, ml], axis=0)

    def out(i, carry):
        at = pl.ds(pl.multiple_of(i * chunk, chunk), chunk)
        ih, il = split2(image_ref[:, at])
        a = jnp.dot(ms, high_ref[:, at], preferred_element_type=F32)
        a = a + jnp.dot(vs, ih, preferred_element_type=F32)
        c = jnp.dot(mh, low_ref[:, at], preferred_element_type=F32)
        c = c + jnp.dot(vh, il, preferred_element_type=F32)
        next_ref[:, at] = a[:width] + a[width:] + c
        return carry

    lax.fori_loop(0, rows // chunk, out, 0)


def call(kernel, out_shape, *args, scratch=(), ident=None, kept=()):
    multi = isinstance(out_shape, (list, tuple))
    spec = pl.BlockSpec(memory_space=pltpu.VMEM)
    return pl.pallas_call(
        kernel,
        out_shape=out_shape,
        in_specs=[
            pl.BlockSpec(memory_space=pltpu.HBM) if i in kept else spec for i in range(len(args))
        ],
        out_specs=tuple([spec] * len(out_shape)) if multi else spec,
        scratch_shapes=list(scratch),
        compiler_params=pltpu.CompilerParams(
            vmem_limit_bytes=40 << 20, collective_id=ident, has_side_effects=ident is not None
        ),
    )(*args)


def shards(
    current, prior, block_values, block_cols, face_match, face_weight,
    fluid_diag, wet_source, wet_dest, wet_target, wet_weight,
):
    high = lax.Precision.HIGH
    width, local_rows = current.shape
    face_rows = face_match.shape[2]
    row_blocks = block_cols.shape[0]
    wet_slots = wet_source.shape[0]
    grp, dev = lax.axis_size("grp"), lax.axis_size("dev")
    subdomains = grp * dev
    total_rows = local_rows * lax.axis_size("sec") * subdomains
    capacity = 2 * wet_slots // subdomains + 8
    per = -(-capacity // LANES)
    slabs = subdomains * per
    is_shell = lax.axis_index("sec") == 0
    flat_prior = prior.reshape(-1, local_rows)
    basis = flat_prior.shape[0]
    n = 2 * subdomains
    stream_scratch = [
        pltpu.VMEM((basis, local_rows), F32),
        pltpu.SemaphoreType.DMA((local_rows // 1024,)),
    ]
    cross, faces, edges, twin = call(
        functools.partial(exchange_kernel, subdomains, face_rows),
        (
            jax.ShapeDtypeStruct((basis, basis), F32),
            jax.ShapeDtypeStruct((ROUNDS, width, face_rows), F32),
            jax.ShapeDtypeStruct((2, width, LANES), F32),
            jax.ShapeDtypeStruct(current.shape, F32),
        ),
        current, flat_prior,
        scratch=[
            pltpu.VMEM((n, basis // n, basis), F32),
            pltpu.VMEM((n, basis // n, basis), F32),
            pltpu.VMEM((n, basis // n, basis), F32),
            pltpu.SemaphoreType.DMA((4,)),
            pltpu.SemaphoreType.DMA((2, ROUNDS)),
            pltpu.SemaphoreType.DMA((2, 2)),
            pltpu.SemaphoreType.DMA((2,)),
            *stream_scratch,
        ],
        ident=0, kept=(1,),
    )
    tiled = (wet_slots // LANES, LANES)
    bands = local_rows // (2 * LANES) * width
    slab = pltpu.VMEM((slabs, width + META, LANES), F32)
    fluid = call(
        functools.partial(wet_kernel, subdomains, per),
        jax.ShapeDtypeStruct((width, local_rows), F32),
        current, twin, fluid_diag[None, :], edges, wet_source.reshape(tiled),
        wet_dest.reshape(tiled), wet_target.reshape(tiled), wet_weight.reshape(tiled),
        scratch=[
            pltpu.VMEM((4, slabs, LANES), F32),
            slab,
            slab,
            pltpu.VMEM((bands, 2 * per * LANES), BF16),
            pltpu.VMEM((bands, 2 * LANES), F32),
            pltpu.SemaphoreType.DMA((2, subdomains)),
        ],
        ident=2,
    )

    def shell_apply(vector):
        picked = vector.reshape(width, row_blocks, BS)[:, block_cols, :]
        matrices = block_values.reshape(row_blocks, NB, BS, BS)
        result = jnp.einsum("kibc,ibrc->kir", picked, matrices, precision=high)
        return call(
            face_kernel, jax.ShapeDtypeStruct((width, local_rows), F32),
            result.reshape(width, local_rows), faces, face_match[0], face_weight[0],
        )

    image = lax.cond(is_shell, shell_apply, lambda x: fluid, current)
    lanes = -(-(basis + width) // LANES) * LANES
    cuts = n // width
    piece = pltpu.VMEM((n, 1, lanes // cuts), F32)
    next_block, coef, factor = call(
        functools.partial(finish_kernel, subdomains, total_rows),
        (
            jax.ShapeDtypeStruct((width, local_rows), F32),
            jax.ShapeDtypeStruct((basis, width), F32),
            jax.ShapeDtypeStruct((width, width), F32),
        ),
        image, flat_prior, cross,
        scratch=[
            pltpu.VMEM((basis, local_rows), BF16),
            pltpu.VMEM((basis, local_rows), BF16),
            piece, piece, piece,
            pltpu.SemaphoreType.DMA((4,)),
            *stream_scratch,
        ],
        ident=1, kept=(1,),
    )
    return (next_block, coef.reshape(prior.shape[0], width, width), factor)


def solution(mesh):
    placed = (
        P(None, ALL),
        P(None, None, ALL),
        P(("grp", "dev"), None, None),
        P(("grp", "dev"), None),
        P(("grp", "dev"), None, None),
        P(("grp", "dev"), None, None),
        P(("grp", "dev")),
        P(("grp", "dev")),
        P(("grp", "dev"), None),
        P(("grp", "dev")),
        P(("grp", "dev")),
    )
    return jax.shard_map(
        shards, mesh=mesh, in_specs=placed, out_specs=(P(None, ALL), P(), P()), check_vma=False
    )
```

profile of v0, /device:TPU:0, one launch (start us, length us, event | category | flops | bytes accessed | tf_op | source)
XLA Modules:
  0.0 106.2 jit_solution(2080030771860973559)
XLA Ops:
  0.7 2.8 %copy-done = f32[8,32,6144]{2,1,0:T(8,128)S(1)} copy-done((f32[8,32,6144]{2,1,0:T(8,128)S(1)}, f32[8,32,6144]{2,1,0:T(8,128)}, u32[]{:S(2)}) %copy-start) | copy-done | bytes 6291480
  3.4 29.2 %shard_map.134 = (f32[256,256]{1,0:T(8,128)S(1)}, f32[4,32,1536]{2,1,0:T(8,128)S(1)}, f32[2,32,128]{2,1,0:T(8,128)S(1)}, f32[32,6144]{1,0:T(8,128)S(1)}) custom-call(f32[32,6144]{1,0:T(8,128)} %x_ref.3, f32[256,6144]{1,0:T(8,128)S(1)} %bitcast.20), custom_call_target="tpu_custom_call" | custom-call | tf_op jit(solution)/shard_map/pallas_call | solution.py:499
  32.7 0.7 copy-done.2
  33.4 0.7 copy-done.3
  34.1 0.7 copy-done.4
  34.9 0.7 copy-done.5
  35.6 0.7 copy-done.6
  36.3 2.4 %shard_map.135 = f32[32,6144]{1,0:T(8,128)} custom-call(f32[32,6144]{1,0:T(8,128)} %x_ref.3, f32[32,6144]{1,0:T(8,128)S(1)} %get-tuple-element.32.xs_ref, f32[1,6144]{1,0:T(1,128)S(1)} %bitcast.23, f32[2,32,128]{2,1,0:T(8,128)S(1)} %get-tuple-element.33.edge_ref, s32[24,128]{1,0:T(8,128)S(1)} %bitcast.24, s32[24,128]{1,0:T(8,128)S(1)} %bitcast.25, ...), custom_call_target="tpu_custom_call" | custom-call | tf_op jit(solution)/shard_map/pallas_call | solution.py:499
  38.7 41.5 %conditional.1 = (f32[32,6144]{1,0:T(8,128)}) conditional(s32[]{:T(128)} %convert_element_type.3, f32[32,6144]{1,0:T(8,128)} %shard_map.135, (f32[32,6144]{1,0:T(8,128)S(1)}, s32[64,6]{0,1:T(8,128)S(1)}, f32[64,6,9216]{2,0,1:T(8,128)}, s32[1,4,1536]{2,1,0:T(4,128)S(1)}, f32[1,4,1536]{2,1,0:T(4,128)S(1)}, /*index=5*/f32[4,32,1536]{2,1,0:T(8,128)S(1)}) %tuple.26), branch_computations={%region_0.0_spmd, %region_1.0_spmd} | conditional | flops 679479424 | bytes 63717384 | solution.py:585
  38.9 0.1 copy.27
  39.0 0.1 reshape.41
  39.2 0.4 reshape.24
  39.6 0.6 copy.24
  40.2 3.8 %gather_fusion = f32[384,32,96]{2,1,0:T(8,128)} fusion(f32[32,64,96]{2,0,1:T(8,128)S(1)} %copy.24, s32[1024]{0:T(1024)S(1)} %pad_clamp_fusion), kind=kCustom, calls=%fused_computation | custom fusion | bytes 9438720 | tf_op jit(solution)/shard_map/cond/branch_1_fun/gather | solution.py:577
  44.0 17.6 %reshape.25 = f32[64,6,96,96]{3,2,0,1:T(8,128)} reshape(f32[64,6,9216]{2,0,1:T(8,128)} %get-tuple-element.44) | data formatting | bytes 28311552 | tf_op jit(solution)/shard_map/cond/branch_1_fun/reshape | solution.py:578
  61.6 13.8 %fusion.2 = f32[32,64,96]{2,0,1:T(8,128)S(1)} fusion(f32[32,64,6,96]{3,0,2,1:T(8,128)} %bitcast.28, f32[64,6,96,96]{3,2,0,1:T(8,128)} %reshape.25), kind=kOutput, calls=%fused_computation.3 | convolution fusion | flops 679477248 | bytes 19660800 | tf_op jit(solution)/shard_map/cond/branch_1_fun/kibc,ibrc->kir/dot_general | solution.py:579
  75.4 0.6 copy.26
  76.0 0.6 reshape.26.y_ref
  76.6 3.6 %branch_1_fun.1 = f32[32,6144]{1,0:T(8,128)} custom-call(f32[32,6144]{1,0:T(8,128)S(1)} %reshape.26.y_ref, f32[4,32,1536]{2,1,0:T(8,128)S(1)} %get-tuple-element.19.faces_ref, s32[4,1536]{1,0:T(4,128)S(1)} %bitcast.29, f32[4,1536]{1,0:T(4,128)S(1)} %bitcast.30), custom_call_target="tpu_custom_call" | custom-call | tf_op jit(solution)/shard_map/cond/branch_1_fun/pallas_call | solution.py:499
  80.3 2.8 %copy-done.1 = f32[8,32,6144]{2,1,0:T(8,128)S(1)} copy-done((f32[8,32,6144]{2,1,0:T(8,128)S(1)}, f32[8,32,6144]{2,1,0:T(8,128)}, u32[]{:S(2)}) %copy-start.1) | copy-done | bytes 6291480
  83.0 21.0 %shard_map.136 = (f32[32,6144]{1,0:T(8,128)S(1)}, f32[256,32]{1,0:T(8,128)S(1)}, f32[32,32]{1,0:T(8,128)S(1)}) custom-call(f32[32,6144]{1,0:T(8,128)} %get-tuple-element.71.image_ref, f32[256,6144]{1,0:T(8,128)S(1)} %bitcast.21, f32[256,256]{1,0:T(8,128)S(1)} %get-tuple-element.35.cross_ref), custom_call_target="tpu_custom_call" | custom-call | tf_op jit(solution)/shard_map/pallas_call | solution.py:499
  104.0 0.9 copy.38
  104.9 0.7 copy.39
  105.6 0.6 copy.40
  (17 shorter events, 0.0 us)
Async XLA Ops:
  0.6 38.0 %copy-start.10 = (s32[64,6]{0,1:T(8,128)S(1)}, s32[64,6]{0,1:T(8,128)}, u32[]{:S(2)}) copy-start(s32[64,6]{0,1:T(8,128)} %param.16) | copy-start | bytes 4612
  0.6 2.8 %copy-start = (f32[8,32,6144]{2,1,0:T(8,128)S(1)}, f32[8,32,6144]{2,1,0:T(8,128)}, u32[]{:S(2)}) copy-start(f32[8,32,6144]{2,1,0:T(8,128)} %param.14) | copy-start | bytes 18874372
  3.4 35.2 %copy-start.7 = (f32[32,6144]{1,0:T(8,128)S(1)}, f32[32,6144]{1,0:T(8,128)}, u32[]{:S(2)}) copy-start(f32[32,6144]{1,0:T(8,128)} %x_ref.3) | copy-start | bytes 2359300
  3.4 35.3 %copy-start.8 = (s32[1,4,1536]{2,1,0:T(4,128)S(1)}, s32[1,4,1536]{2,1,0:T(4,128)}, u32[]{:S(2)}) copy-start(s32[1,4,1536]{2,1,0:T(4,128)} %param.17) | copy-start | bytes 73732
  3.4 35.3 %copy-start.9 = (f32[1,4,1536]{2,1,0:T(4,128)S(1)}, f32[1,4,1536]{2,1,0:T(4,128)}, u32[]{:S(2)}) copy-start(f32[1,4,1536]{2,1,0:T(4,128)} %param.18) | copy-start | bytes 73732
  32.7 0.7 copy-start.2
  33.4 0.7 copy-start.3
  34.1 0.7 copy-start.4
  34.9 0.7 copy-start.5
  35.6 0.7 copy-start.6
  80.3 2.8 %copy-start.1 = (f32[8,32,6144]{2,1,0:T(8,128)S(1)}, f32[8,32,6144]{2,1,0:T(8,128)}, u32[]{:S(2)}) copy-start(f32[8,32,6144]{2,1,0:T(8,128)} %param.14) | copy-start | bytes 18874372
where the time goes:
time: 107 us; the launch traced here: 106 us
  Pallas kernels  56.3 us (53%)
  local copies, waits for them, and re-layouts  35.1 us (33%)
  matrix products  13.8 us (13%)
    pallas_call x4, Pallas kernels, call(): pl.pallas_call(kernel, out_shape=out_shape, in_specs=[pl.BlockSpec(memory...  56.3 us
    reshape x1, local copies, waits for them, and re-layouts, shell_apply(): matrices = block_values.reshape(row_blocks, NB, BS, BS)  17.6 us
    dot_general x1, matrix products, shell_apply(): result = jnp.einsum('kibc,ibrc->kir', picked, matrices, precision=high)  13.8 us
    unnamed x25, local copies, waits for them, and re-layouts  11.3 us
    gather x1, local copies, waits for them, and re-layouts, shell_apply(): picked = vector.reshape(width, row_blocks, BS)[:, block_cols, :]  3.76 us

commit v1 on v0

v1 whole, which is shorter than its diff:
```python
import functools

import jax
import jax.numpy as jnp
from jax import lax
from jax.experimental import pallas as pl
from jax.experimental.pallas import tpu as pltpu
from jax.sharding import PartitionSpec as P

BS = 96
NB = 6
ROUNDS = 4
LANES = 128
META = 8
PART = 32
F32 = jnp.float32
BF16 = jnp.bfloat16
NT = (((1,), (1,)), ((), ()))
ALL = ("sec", "grp", "dev")


def split2(x):
    hi = x.astype(BF16)
    return hi, (x - hi.astype(F32)).astype(BF16)


def nt(a, b):
    return lax.dot_general(a, b, NT, preferred_element_type=F32)


def lane_gather(x, low):
    return jnp.take_along_axis(x, low, axis=1)


def wet_sort(subdomains, per, src_ref, dest_ref, tgt_ref, w_ref, meta_ref):
    blocks = src_ref.shape[0]
    slabs = subdomains * per
    dest = dest_ref[...]
    lane = lax.broadcasted_iota(jnp.int32, (LANES, LANES), 1)
    sub = lax.broadcasted_iota(jnp.int32, (LANES, LANES), 0)
    tri = jnp.where(sub < lane, 1.0, 0.0).astype(BF16)
    ones = jnp.ones((LANES, LANES), BF16)
    low_tri = jnp.where(
        lax.broadcasted_iota(jnp.int32, (blocks, blocks), 1)
        < lax.broadcasted_iota(jnp.int32, (blocks, blocks), 0),
        1.0,
        0.0,
    ).astype(BF16)

    def count(q, rank):
        mine = dest == q
        oh = jnp.where(mine, 1.0, 0.0).astype(BF16)
        within = jnp.dot(oh, tri, preferred_element_type=F32)
        totals = jnp.dot(oh, ones, preferred_element_type=F32).astype(BF16)
        offset = jnp.dot(low_tri, totals, preferred_element_type=F32)
        return jnp.where(mine, within + offset, rank)

    rank = lax.fori_loop(0, subdomains, count, jnp.zeros(dest.shape, F32)).astype(jnp.int32)
    slab = dest * per + rank // LANES
    spot = rank % LANES
    src = src_ref[...]
    tgt = tgt_ref[...]
    w = w_ref[...]
    w0 = w.astype(BF16).astype(F32)
    w1 = (w - w0).astype(BF16).astype(F32)
    w2 = w - w0 - w1
    fields = [src // LANES, src % LANES, tgt // LANES, tgt % LANES]
    fields = [f.astype(F32) for f in fields] + [w0, w1, w2]
    acc = jnp.zeros((len(fields) * slabs, LANES), F32)
    slab_row = lax.broadcasted_iota(jnp.int32, (slabs, LANES), 0)
    for i in range(blocks):
        hit = slab_row == slab[i : i + 1, :]
        lhs = jnp.concatenate([jnp.where(hit, f[i : i + 1, :], 0.0) for f in fields], axis=0)
        oh = jnp.where(sub == spot[i : i + 1, :], 1.0, 0.0)
        acc = acc + nt(lhs.astype(BF16), oh.astype(BF16))
    parts = [acc[f * slabs : (f + 1) * slabs] for f in range(len(fields))]
    meta_ref[0] = parts[0]
    meta_ref[1] = parts[1]
    meta_ref[2] = parts[2] * LANES + parts[3]
    meta_ref[3] = parts[4] + parts[5] + parts[6]


class Wet:
    def __init__(self, subdomains, per, mine, x_ref, meta_ref, pack_ref, got_ref, lhs_ref, acc_ref, sems):
        self.subdomains, self.per, self.mine, self.x_ref, self.meta_ref = subdomains, per, mine, x_ref, meta_ref
        self.pack_ref, self.got_ref, self.lhs_ref, self.acc_ref, self.sems = pack_ref, got_ref, lhs_ref, acc_ref, sems
        self.width, self.rows = x_ref.shape

    def gather(self, a, ref, to):
        width, row = self.width, pl.ds(a, 1)
        high = jnp.broadcast_to(self.meta_ref[0, row, :].astype(jnp.int32), (width, LANES))
        low = jnp.broadcast_to(self.meta_ref[1, row, :].astype(jnp.int32), (width, LANES))
        got = jnp.zeros((width, LANES), F32)
        for h in range(self.rows // LANES):
            piece = lane_gather(self.x_ref[:, h * LANES : (h + 1) * LANES], low)
            got = jnp.where(high == h, piece, got)
        ref[to, :width, :] = got * self.meta_ref[3, row, :]
        ref[to, width:, :] = jnp.broadcast_to(self.meta_ref[2, row, :], (META, LANES))

    def copy(self, to, at):
        per = self.per
        return remote(
            self.pack_ref.at[pl.ds(to * per, per)], self.got_ref.at[pl.ds(at * per, per)], self.sems.at[0, to],
            self.sems.at[1, at], place(self.subdomains + to),
        )

    def send(self, first, last):
        per, mine = self.per, self.mine

        def body(s, carry):
            q = lax.rem(mine + s, self.subdomains)

            def one(p, inner):
                self.gather(q * per + p, self.pack_ref, q * per + p)
                return inner

            lax.fori_loop(0, per, one, 0)
            self.copy(q, mine).start()
            return carry

        lax.fori_loop(first, last, body, 0)

    def keep(self):
        def one(p, inner):
            self.gather(self.mine * self.per + p, self.got_ref, self.mine * self.per + p)
            return inner

        lax.fori_loop(0, self.per, one, 0)

    def add(self, q):
        width, wide = self.width, 2 * LANES
        highs = self.rows // wide
        got_ref, lhs_ref = self.got_ref, self.lhs_ref
        ohs = []
        for s in range(self.per):
            a = q * self.per + s
            target = got_ref[a, width : width + 1, :].astype(jnp.int32)
            vals = got_ref[a, :width, :]
            hi = vals.astype(BF16).astype(F32)
            lo = vals - hi
            high = jnp.broadcast_to(target // wide, (width, LANES))
            low = target % wide
            at = s * wide
            for h in range(highs):
                hit = high == h
                band = slice(h * width, (h + 1) * width)
                lhs_ref[band, at : at + LANES] = jnp.where(hit, hi, 0.0).astype(BF16)
                lhs_ref[band, at + LANES : at + wide] = jnp.where(hit, lo, 0.0).astype(BF16)
            oh = jnp.where(
                lax.broadcasted_iota(jnp.int32, (wide, LANES), 0) == low, 1.0, 0.0
            ).astype(BF16)
            ohs += [oh, oh]
        self.acc_ref[...] += nt(lhs_ref[...], jnp.concatenate(ohs, axis=1))

    def receive(self):
        subdomains, mine = self.subdomains, self.mine
        self.acc_ref[...] = jnp.zeros_like(self.acc_ref)
        self.add(mine)

        def take(s, carry):
            q = lax.rem(mine + subdomains - s, subdomains)
            self.copy(q, q).wait_recv()
            self.add(q)
            return carry

        lax.fori_loop(1, subdomains, take, 0)

    def drain(self):
        def body(s, carry):
            self.copy(lax.rem(self.mine + s, self.subdomains), self.mine).wait_send()
            return carry

        lax.fori_loop(1, self.subdomains, body, 0)


def fluid_image(mine, subdomains, own_ref, diag_ref, edge_ref, acc_ref, image_ref):
    width, rows = own_ref.shape
    edges = [
        jnp.where(mine == 0, 0.0, edge_ref[0]),
        jnp.where(mine == subdomains - 1, 0.0, edge_ref[1]),
    ]
    lane = lax.broadcasted_iota(jnp.int32, (width, LANES), 1)
    pieces = rows // LANES
    for t in range(pieces):
        own = own_ref[:, t * LANES : (t + 1) * LANES]
        prev = edges[0] if t == 0 else own_ref[:, (t - 1) * LANES : t * LANES]
        nxt = edges[1] if t == pieces - 1 else own_ref[:, (t + 1) * LANES : (t + 2) * LANES]
        before = jnp.where(lane == 0, pltpu.roll(prev, 1, 1), pltpu.roll(own, 1, 1))
        after = jnp.where(
            lane == LANES - 1, pltpu.roll(nxt, LANES - 1, 1), pltpu.roll(own, LANES - 1, 1)
        )
        h, side = t // 2, t % 2
        added = acc_ref[h * width : (h + 1) * width, side * LANES : (side + 1) * LANES]
        d = diag_ref[:, t * LANES : (t + 1) * LANES]
        image_ref[:, t * LANES : (t + 1) * LANES] = d * own - before - after + added


def stack_terms(hi, lo):
    zero = jnp.zeros_like(hi)
    return jnp.concatenate([hi, lo, zero, zero, zero, zero, hi, lo], axis=0)


def shell_prepare(x_ref, left_ref, right_ref):
    lanes = lax.broadcasted_iota(jnp.int32, (LANES, LANES), 1)
    subs = lax.broadcasted_iota(jnp.int32, (LANES, LANES), 0)
    eye = jnp.where(lanes == subs, 1.0, 0.0).astype(BF16)

    def body(t, carry):
        at = pl.ds(pl.multiple_of(t * LANES, LANES), LANES)
        v = x_ref[:, at]
        hi = v.astype(BF16).astype(F32)
        both = nt(eye, stack_terms(hi, v - hi).astype(BF16)).astype(BF16)
        to = pl.ds(t * (LANES // PART), LANES // PART)
        left_ref[to] = both[:, :LANES].reshape(LANES // PART, PART, LANES)
        right_ref[to] = both[:, LANES:].reshape(LANES // PART, PART, LANES)
        return carry

    lax.fori_loop(0, x_ref.shape[1] // LANES, body, 0)


def shell_rows(group, cols_ref, blocks_ref, left_ref, right_ref, even_ref, odd_ref):
    chunks = BS * BS // LANES
    high = chunks // 3
    lane = lax.broadcasted_iota(jnp.int32, (high, LANES), 1)
    first = lane % (LANES // 2) < LANES // 4
    front = lane < LANES // 2
    for r in range(8):
        row = group * 8 + r
        at = [cols_ref[row, b] * (BS // PART) for b in range(NB)]
        outs = []
        for s in range(3):
            v = jnp.concatenate(
                [
                    blocks_ref[b, pl.ds(group * chunks * 8 + 8 * s + r, high, stride=24), :]
                    for b in range(NB)
                ],
                axis=1,
            )
            hi = v.astype(BF16).astype(F32)
            lhs = jnp.concatenate([hi, v - hi], axis=0).astype(BF16)
            spans = (
                ((left_ref, 0), (left_ref, 1), (left_ref, 2), (right_ref, 0)),
                ((right_ref, 1), (right_ref, 2), (left_ref, 0), (left_ref, 1)),
                ((left_ref, 2), (right_ref, 0), (right_ref, 1), (right_ref, 2)),
            )[s]
            rhs = jnp.concatenate([ref[at[b] + o] for b in range(NB) for ref, o in spans], axis=0)
            outs.append(jnp.dot(lhs, rhs, preferred_element_type=F32))

        def fold(z):
            return z[:high] + jnp.where(first, z[high:], 0.0)

        u = [fold(z) for z in outs]
        to = pl.ds(pl.multiple_of(row * high, 8), high)
        even_ref[to, :] = u[0] + jnp.where(front, 0.0, u[1])
        odd_ref[to, :] = u[2] + jnp.where(front, u[1], 0.0)


def shell_store(even_ref, odd_ref, out_ref):
    width = out_ref.shape[0]
    lane = lax.broadcasted_iota(jnp.int32, (width, LANES), 1)
    phase = lane % 4

    def body(t, carry):
        at = pl.ds(pl.multiple_of(t * LANES, LANES), LANES)
        even, odd = even_ref[at, :].T, odd_ref[at, :].T
        y = [
            even[:width] + even[width : 2 * width],
            even[2 * width : 3 * width] + even[3 * width :],
            odd[:width] + odd[width : 2 * width],
            odd[2 * width : 3 * width] + odd[3 * width :],
        ]
        for o in range(4):
            index = lane // 4 + 32 * o
            g = [lane_gather(v, index) for v in y]
            got = jnp.where(phase == 0, g[0], jnp.where(phase == 1, g[1], jnp.where(phase == 2, g[2], g[3])))
            out_ref[:, pl.ds(pl.multiple_of(t * 4 * LANES, LANES) + o * LANES, LANES)] = got
        return carry

    lax.fori_loop(0, even_ref.shape[0] // LANES, body, 0)


def add_faces(faces_ref, match_ref, weight_ref, out_ref):
    width = out_ref.shape[0]
    rounds, face = match_ref.shape
    pieces = face // LANES
    for m in range(rounds):
        for o in range(pieces):
            index = match_ref[m : m + 1, o * LANES : (o + 1) * LANES]
            high = jnp.broadcast_to(index // LANES, (width, LANES))
            low = jnp.broadcast_to(index % LANES, (width, LANES))
            got = jnp.zeros((width, LANES), F32)
            for h in range(pieces):
                piece = lane_gather(faces_ref[m, :, h * LANES : (h + 1) * LANES], low)
                got = jnp.where(high == h, piece, got)
            at = m * face + o * LANES
            w = weight_ref[m : m + 1, o * LANES : (o + 1) * LANES]
            out_ref[:, at : at + LANES] += w * got


MESH = pl.DeviceIdType.MESH


def place(index):
    dev = lax.axis_size("dev")
    grp = lax.axis_size("grp")
    return (index // (grp * dev), index // dev % grp, index % dev)


def turns(axis):
    count = lax.axis_size(axis)
    ring = [lax.axis_index(axis)]
    for _ in range(1, count):
        following = ring[-1] + 1
        ring.append(jnp.where(following == count, 0, following))
    return ring


def announce():
    barrier = pltpu.get_barrier_semaphore()
    rings = [turns(axis) for axis in ALL]
    for i, s in enumerate(rings[0]):
        for j, g in enumerate(rings[1]):
            for k, d in enumerate(rings[2]):
                if i or j or k:
                    pl.semaphore_signal(barrier, inc=1, device_id=(s, g, d), device_id_type=MESH)
    return barrier


def remote(src, dst, send, recv, device):
    return pltpu.make_async_remote_copy(
        src_ref=src, dst_ref=dst, send_sem=send, recv_sem=recv, device_id=device,
        device_id_type=MESH,
    )


class Reduce:
    def __init__(self, stage, slots, along, total, sems):
        self.stage, self.slots, self.along, self.total, self.sems = stage, slots, along, total, sems
        self.sec, self.g, self.d = (lax.axis_index(axis) for axis in ALL)
        self.grp = lax.axis_size("grp")
        self.me = self.sec * self.grp + self.g

    def plane(self, body):
        for i, s in enumerate(turns("sec")):
            for j, g in enumerate(turns("grp")):
                if i or j:
                    body(s * self.grp + g, (s, g, self.d))

    def bulk(self, source, target, first):
        rest = pl.ds(0, source.shape[0] - 1)
        other = (1 - self.sec, self.g, self.d)
        return remote(source.at[rest], target.at[rest], self.sems.at[first], self.sems.at[first + 1], other)

    def scatter(self):
        self.plane(
            lambda p, where: remote(
                self.stage.at[p], self.slots.at[self.me], self.sems.at[0], self.sems.at[1], where
            ).start()
        )

    def middle(self):
        self.bulk(self.stage, self.slots, 0).wait_recv()
        self.slots[self.me] = self.stage[self.me]
        self.along[self.d] = jnp.sum(self.slots[...], axis=0)
        for d in turns("dev")[1:]:
            remote(
                self.along.at[self.d], self.along.at[self.d], self.sems.at[2], self.sems.at[3],
                (self.sec, self.g, d),
            ).start()

    def gather(self):
        self.bulk(self.along, self.along, 2).wait_recv()
        self.total[self.me] = jnp.sum(self.along[...], axis=0)
        self.plane(
            lambda p, where: remote(
                self.total.at[self.me], self.total.at[self.me], self.sems.at[4], self.sems.at[5], where
            ).start()
        )

    def finish(self):
        self.bulk(self.total, self.total, 4).wait_recv()

    def drain(self):
        self.bulk(self.stage, self.slots, 0).wait_send()
        self.bulk(self.along, self.along, 2).wait_send()
        self.bulk(self.total, self.total, 4).wait_send()


def step_kernel(names, subdomains, per, total_rows, *refs):
    r = dict(zip(names, refs))
    n = 2 * subdomains
    sec, g, d = (lax.axis_index(axis) for axis in ALL)
    mine = g * lax.axis_size("dev") + d
    x_ref, image_ref = r["x"], r["image"]
    width, rows = x_ref.shape
    face = r["match"].shape[1]
    held, high_ref, low_ref = r["held"], r["high"], r["low"]
    basis = held.shape[0]
    chunk = rows // r["held_sems"].shape[0]
    groups = r["block_sems"].shape[0]

    def local(name, i):
        return pltpu.make_async_copy(r[name + "_hbm"], r[name], r["local_sems"].at[i])

    def prior_copy(i):
        at = pl.ds(pl.multiple_of(i * chunk, chunk), chunk)
        return pltpu.make_async_copy(r["prior_hbm"].at[:, at], held.at[:, at], r["held_sems"].at[i])

    def block_copy(i):
        span = r["blocks"].shape[1] // groups
        at = pl.ds(pl.multiple_of(i * span, 8), span)
        return pltpu.make_async_copy(r["blocks_hbm"].at[:, at], r["blocks"].at[:, at], r["block_sems"].at[i])

    structure = ("match", "weight")
    fluid = ("src", "dest", "tgt", "w", "diag")
    local("x", 0).start()

    @pl.when(sec == 1)
    def _():
        for i, name in enumerate(fluid):
            local(name, 1 + i).start()

    for i in range(rows // chunk):
        prior_copy(i).start()

    @pl.when(sec == 0)
    def _():
        for i in range(groups):
            block_copy(i).start()
        for i, name in enumerate(structure):
            local(name, 1 + i).start()

    barrier = announce()
    local("x", 0).wait()

    @pl.when(sec == 0)
    def _():
        shell_prepare(x_ref, r["left"], r["right"])

    @pl.when(sec == 1)
    def _():
        for i, name in enumerate(fluid):
            local(name, 1 + i).wait()
        wet_sort(subdomains, per, r["src"], r["dest"], r["tgt"], r["w"], r["meta"])

    pl.semaphore_wait(barrier, n - 1)
    partners = [
        (0, g, d + 1 - 2 * lax.rem(d, 2)),
        (0, g, d + 2 - 4 * lax.rem(d // 2, 2)),
        (0, g + 1 - 2 * lax.rem(g, 2), d),
        (0, g + 2 - 4 * lax.rem(g // 2, 2), d),
    ]

    def face_copy(m):
        return remote(
            x_ref.at[:, pl.ds(m * face, face)], r["faces"].at[m], r["face_sems"].at[0, m],
            r["face_sems"].at[1, m], partners[m],
        )

    def edge_copy(side):
        to = subdomains + lax.rem(mine + (1 if side == 0 else subdomains - 1), subdomains)
        at = rows - LANES if side == 0 else 0
        return remote(
            x_ref.at[:, pl.ds(at, LANES)], r["edge"].at[side], r["edge_sems"].at[0, side],
            r["edge_sems"].at[1, side], place(to),
        )

    def twin_copy():
        return remote(x_ref, r["xs"], r["twin_sems"].at[0], r["twin_sems"].at[1], (1, g, d))

    @pl.when(sec == 0)
    def _():
        twin_copy().start()
        for m in range(ROUNDS):
            face_copy(m).start()

    @pl.when(sec == 1)
    def _():
        edge_copy(0).start()
        edge_copy(1).start()

    def product(i, carry):
        same, mixed = carry
        prior_copy(i).wait()
        at = pl.ds(pl.multiple_of(i * chunk, chunk), chunk)
        hi, lo = split2(held[:, at])
        high_ref[:, at] = hi
        low_ref[:, at] = lo
        return same + nt(hi, hi), mixed + nt(hi, lo)

    zero = jnp.zeros((basis, basis), F32)
    same, mixed = lax.fori_loop(0, rows // chunk, product, (zero, zero))
    part = same + mixed + mixed.T
    cross_sum = Reduce(r["g_stage"], r["g_slots"], r["g_along"], r["g_total"], r["g_sems"])
    cross_sum.stage[...] = part.reshape(cross_sum.stage.shape)
    cross_sum.scatter()
    wet = Wet(
        subdomains, per, mine, r["xs"], r["meta"], r["pack"], r["got"], r["lhs"], r["acc"], r["wet_sems"]
    )

    def shell(first, last):
        def body(i, carry):
            block_copy(i).wait()
            shell_rows(i, r["cols"], r["blocks"], r["left"], r["right"], r["even"], r["odd"])
            return carry

        lax.fori_loop(first, last, body, 0)

    @pl.when(sec == 0)
    def _():
        shell(0, groups // 2)

    @pl.when(sec == 1)
    def _():
        twin_copy().wait_recv()
        wet.send(1, subdomains // 2)

    cross_sum.middle()

    @pl.when(sec == 0)
    def _():
        shell(groups // 2, groups)

    @pl.when(sec == 1)
    def _():
        wet.send(subdomains // 2, subdomains)
        wet.keep()

    cross_sum.gather()

    @pl.when(sec == 0)
    def _():
        shell_store(r["even"], r["odd"], image_ref)
        for i, name in enumerate(structure):
            local(name, 1 + i).wait()
        for m in range(ROUNDS):
            face_copy(m).wait()
        add_faces(r["faces"], r["match"], r["weight"], image_ref)
        twin_copy().wait_send()

    @pl.when(sec == 1)
    def _():
        wet.receive()
        edge_copy(0).wait()
        edge_copy(1).wait()
        fluid_image(mine, subdomains, x_ref, r["diag"], r["edge"], r["acc"], image_ref)
        wet.drain()

    ih, il = split2(image_ref[...])
    both = nt(jnp.concatenate([ih, il], axis=0), high_ref[...])
    head = both[:width] + both[width:] + nt(ih, low_ref[...])
    mixed = nt(ih, il)
    square = nt(ih, ih) + mixed + mixed.T
    part = jnp.concatenate(
        [head, square, jnp.zeros((width, -(basis + width) % LANES), F32)], axis=1
    )
    head_sum = Reduce(r["h_stage"], r["h_slots"], r["h_along"], r["h_total"], r["h_sems"])
    count, piece = head_sum.stage.shape[:2]
    for i in range(count):
        head_sum.stage[i] = part[i * piece : (i + 1) * piece]
    head_sum.scatter()
    cross_sum.finish()
    cross_sum.drain()
    head_sum.middle()
    head_sum.gather()
    head_sum.finish()
    head_sum.drain()
    cross = cross_sum.total[...].reshape(basis, basis)
    summed = jnp.concatenate([head_sum.total[i] for i in range(count)], axis=0)
    first = summed[:, :basis]
    square = summed[:, basis : basis + width]
    highest = lax.Precision.HIGHEST

    def dot(a, b):
        return jnp.dot(a, b, precision=highest, preferred_element_type=F32)

    def dot_nt(a, b):
        return lax.dot_general(a, b, NT, precision=highest, preferred_element_type=F32)

    coef = 2.0 * first - dot(first, cross)
    gram = (
        square - dot_nt(coef, first) - dot_nt(first, coef) + dot_nt(dot(coef, cross), coef)
    ) * (1.0 / total_rows)
    r["coef"][...] = coef.T
    sub = lax.broadcasted_iota(jnp.int32, (width, 2 * width), 0)
    lane = lax.broadcasted_iota(jnp.int32, (width, 2 * width), 1)
    eye = jnp.where(sub + width == lane, 1.0, 0.0)
    work = jnp.concatenate([gram, jnp.zeros((width, width), F32)], axis=1) + eye
    for j in range(width):
        root = jnp.sqrt(work[j : j + 1, j : j + 1])
        row = work[j : j + 1, :] / root
        column = work[:, j : j + 1] / root
        work = jnp.where(sub == j, row, jnp.where(sub > j, work - column * row, work))
    r["fac"][...] = jnp.where(sub <= lane, work, 0.0)[:, :width]
    inverse = work[:, width:]
    mix = -dot(inverse, coef)
    vh, vl = split2(inverse)
    mh, ml = split2(mix)
    vs = jnp.concatenate([vh, vl], axis=0)
    ms = jnp.concatenate([mh, ml], axis=0)

    def out(i, carry):
        at = pl.ds(pl.multiple_of(i * chunk, chunk), chunk)
        ih, il = split2(image_ref[:, at])
        a = jnp.dot(ms, high_ref[:, at], preferred_element_type=F32)
        a = a + jnp.dot(vs, ih, preferred_element_type=F32)
        c = jnp.dot(mh, low_ref[:, at], preferred_element_type=F32)
        c = c + jnp.dot(vh, il, preferred_element_type=F32)
        r["next"][:, at] = a[:width] + a[width:] + c
        return carry

    lax.fori_loop(0, rows // chunk, out, 0)


def shards(
    current, prior, block_values, block_cols, face_match, face_weight,
    fluid_diag, wet_source, wet_dest, wet_target, wet_weight,
):
    width, local_rows = current.shape
    face_rows = face_match.shape[2]
    row_blocks = block_cols.shape[0]
    wet_slots = wet_source.shape[0]
    grp, dev = lax.axis_size("grp"), lax.axis_size("dev")
    subdomains = grp * dev
    total_rows = local_rows * lax.axis_size("sec") * subdomains
    capacity = 2 * wet_slots // subdomains + 8
    per = -(-capacity // LANES)
    slabs = subdomains * per
    flat_prior = prior.reshape(-1, local_rows)
    basis = flat_prior.shape[0]
    plane = 2 * grp
    group = row_blocks // 8
    tiles = block_values.transpose(1, 0, 2).reshape(NB, group, 8, BS * BS // LANES, LANES)
    tiles = tiles.transpose(0, 1, 3, 2, 4).reshape(NB, row_blocks * BS * BS // LANES, LANES)
    tiled = (wet_slots // LANES, LANES)
    any_spec, smem = pl.BlockSpec(memory_space=pl.ANY), pl.BlockSpec(memory_space=pltpu.SMEM)
    spec = pl.BlockSpec(memory_space=pltpu.VMEM)
    inputs = {
        "x_hbm": current, "prior_hbm": flat_prior, "blocks_hbm": tiles, "cols": block_cols,
        "match_hbm": face_match[0], "weight_hbm": face_weight[0], "diag_hbm": fluid_diag[None, :],
        "src_hbm": wet_source.reshape(tiled), "dest_hbm": wet_dest.reshape(tiled),
        "tgt_hbm": wet_target.reshape(tiled), "w_hbm": wet_weight.reshape(tiled),
    }
    outputs = {
        "next": jax.ShapeDtypeStruct((width, local_rows), F32),
        "coef": jax.ShapeDtypeStruct((basis, width), F32),
        "fac": jax.ShapeDtypeStruct((width, width), F32),
    }
    lanes = -(-(basis + width) // LANES) * LANES
    slab = pltpu.VMEM((slabs, width + META, LANES), F32)
    bands = local_rows // (2 * LANES) * width
    field = pltpu.VMEM((width, local_rows), F32)
    cross_piece = pltpu.VMEM((plane, basis // plane, basis), F32)
    head_piece = pltpu.VMEM((plane, width // plane, lanes), F32)
    dma = pltpu.SemaphoreType.DMA
    scratch = {
        "image": field, "x": field, "xs": field,
        "held": pltpu.VMEM((basis, local_rows), F32),
        "high": pltpu.VMEM((basis, local_rows), BF16), "low": pltpu.VMEM((basis, local_rows), BF16),
        "blocks": pltpu.VMEM(tiles.shape, F32),
        "left": pltpu.VMEM((local_rows // PART, PART, LANES), BF16),
        "right": pltpu.VMEM((local_rows // PART, PART, LANES), BF16),
        "even": pltpu.VMEM((local_rows // 4, LANES), F32), "odd": pltpu.VMEM((local_rows // 4, LANES), F32),
        "faces": pltpu.VMEM((ROUNDS, width, face_rows), F32),
        "edge": pltpu.VMEM((2, width, LANES), F32),
        "match": pltpu.VMEM((ROUNDS, face_rows), jnp.int32), "weight": pltpu.VMEM((ROUNDS, face_rows), F32),
        "diag": pltpu.VMEM((1, local_rows), F32),
        "src": pltpu.VMEM(tiled, jnp.int32), "dest": pltpu.VMEM(tiled, jnp.int32),
        "tgt": pltpu.VMEM(tiled, jnp.int32), "w": pltpu.VMEM(tiled, F32),
        "meta": pltpu.VMEM((4, slabs, LANES), F32),
        "pack": slab, "got": slab,
        "lhs": pltpu.VMEM((bands, 2 * per * LANES), BF16), "acc": pltpu.VMEM((bands, 2 * LANES), F32),
        "g_stage": cross_piece, "g_slots": cross_piece, "g_total": cross_piece,
        "g_along": pltpu.VMEM((dev, basis // plane, basis), F32),
        "h_stage": head_piece, "h_slots": head_piece, "h_total": head_piece,
        "h_along": pltpu.VMEM((dev, width // plane, lanes), F32),
        "local_sems": dma((6,)), "held_sems": dma((local_rows // 1024,)), "block_sems": dma((group,)),
        "face_sems": dma((2, ROUNDS)), "edge_sems": dma((2, 2)), "twin_sems": dma((2,)),
        "wet_sems": dma((2, subdomains)), "g_sems": dma((6,)), "h_sems": dma((6,)),
    }
    names = (*inputs, *outputs, *scratch)
    next_block, coef, factor = pl.pallas_call(
        functools.partial(step_kernel, names, subdomains, per, total_rows),
        out_shape=tuple(outputs.values()),
        in_specs=[smem if name == "cols" else any_spec for name in inputs],
        out_specs=(spec,) * len(outputs),
        scratch_shapes=list(scratch.values()),
        compiler_params=pltpu.CompilerParams(
            vmem_limit_bytes=60 << 20, collective_id=0, has_side_effects=True
        ),
    )(*inputs.values())
    return (next_block, coef.reshape(prior.shape[0], width, width), factor)


def solution(mesh):
    placed = (
        P(None, ALL),
        P(None, None, ALL),
        P(("grp", "dev"), None, None),
        P(("grp", "dev"), None),
        P(("grp", "dev"), None, None),
        P(("grp", "dev"), None, None),
        P(("grp", "dev")),
        P(("grp", "dev")),
        P(("grp", "dev"), None),
        P(("grp", "dev")),
        P(("grp", "dev")),
    )
    return jax.shard_map(
        shards, mesh=mesh, in_specs=placed, out_specs=(P(None, ALL), P(), P()), check_vma=False
    )
```

time: 107 us -> 72.6 us (0.68)
  local copies, waits for them, and re-layouts: 35.1 us -> 6.34 us
  matrix products: 13.8 us -> 0 us
  Pallas kernels: 56.3 us -> 65.3 us
    reshape x4 -> x0, local copies, waits for them, and re-layouts: 19.3 us -> none  [the longest x1 17.6 us: shell_apply(): matrices = block_values.reshape(row_blocks, NB, BS, BS)]
    dot_general x1 -> x0, matrix products: 13.8 us -> none  [shell_apply(): result = jnp.einsum('kibc,ibrc->kir', picked, matrices, precision=high)]
    pallas_call x4 -> x1, Pallas kernels: 56.3 us -> 65.3 us  [shards(): pl.pallas_call(functools.partial(step_kernel, names, subdomains, per, tot...]
    unnamed x25 -> x4, local copies, waits for them, and re-layouts: 11.3 us -> 6.34 us
    gather x1 -> x0, local copies, waits for them, and re-layouts: 3.76 us -> none  [shell_apply(): picked = vector.reshape(width, row_blocks, BS)[:, block_cols, :]]
where the time goes in v1:
time: 72.6 us; the launch traced here: 72.3 us
  Pallas kernels  65.3 us (90%)
  local copies, waits for them, and re-layouts  6.34 us (9%)
    pallas_call x1, Pallas kernels, shards(): pl.pallas_call(functools.partial(step_kernel, names, subdomains, per, tot...  65.3 us
    unnamed x4, local copies, waits for them, and re-layouts  6.34 us

profile of v1, /device:TPU:0, one launch (start us, length us, event | category | flops | bytes accessed | tf_op | source)
XLA Modules:
  0.0 72.3 jit_solution(10624008649418444037)
XLA Ops:
  0.6 1.4 %copy.14.refs_3_ = s32[64,6]{1,0:T(8,128)} copy(s32[64,6]{0,1:T(8,128)} %param.14) | data formatting | bytes 3072 | tf_op args[3]
  2.0 65.3 %shard_map.130 = (f32[32,6144]{1,0:T(8,128)}, f32[256,32]{1,0:T(8,128)}, f32[32,32]{1,0:T(8,128)}) custom-call(f32[32,6144]{1,0:T(8,128)} %refs_0_.1, f32[256,6144]{1,0:T(8,128)} %bitcast.17, f32[6,4608,128]{2,1,0:T(8,128)} %bitcast.16, s32[64,6]{1,0:T(8,128)} %copy.14.refs_3_, s32[4,1536]{1,0:T(4,128)} %bitcast.19, f32[4,1536]{1,0:T(4,128)} %bitcast.20, ...), custom_call_target="tpu_custom_call" | custom-call | tf_op jit(solution)/shard_map/pallas_call | solution.py:682
  67.3 2.1 %copy.18 = f32[32,6144]{1,0:T(8,128)} copy(f32[32,6144]{1,0:T(8,128)} %get-tuple-element.12) | data formatting | bytes 1572864
  69.4 1.6 %copy.19 = f32[8,32,32]{2,1,0:T(8,128)} copy(f32[8,32,32]{2,1,0:T(8,128)} %bitcast.18) | data formatting | bytes 65536
  70.9 1.3 %copy.20 = f32[32,32]{1,0:T(8,128)} copy(f32[32,32]{1,0:T(8,128)} %get-tuple-element.14) | data formatting | bytes 8192

commit v2 on v1

--- a/solution.py
+++ b/solution.py
@@ -11,7 +11,7 @@
 NB = 6
 ROUNDS = 4
 LANES = 128
-META = 8
+QUAD = 4
 PART = 32
 F32 = jnp.float32
 BF16 = jnp.bfloat16
@@ -32,9 +32,10 @@
     return jnp.take_along_axis(x, low, axis=1)
 
 
-def wet_sort(subdomains, per, src_ref, dest_ref, tgt_ref, w_ref, meta_ref):
+def wet_sort(subdomains, limit, src_ref, dest_ref, tgt_ref, w_ref, index_ref, pack_ref):
     blocks = src_ref.shape[0]
-    slabs = subdomains * per
+    slabs = subdomains * QUAD
+    top = pack_ref.shape[1] - 2 * QUAD
     dest = dest_ref[...]
     lane = lax.broadcasted_iota(jnp.int32, (LANES, LANES), 1)
     sub = lax.broadcasted_iota(jnp.int32, (LANES, LANES), 0)
@@ -56,8 +57,8 @@
         return jnp.where(mine, within + offset, rank)
 
     rank = lax.fori_loop(0, subdomains, count, jnp.zeros(dest.shape, F32)).astype(jnp.int32)
-    slab = dest * per + rank // LANES
-    spot = rank % LANES
+    slab = dest * QUAD + rank % QUAD
+    spot = rank // QUAD
     src = src_ref[...]
     tgt = tgt_ref[...]
     w = w_ref[...]
@@ -74,96 +75,112 @@
         oh = jnp.where(sub == spot[i : i + 1, :], 1.0, 0.0)
         acc = acc + nt(lhs.astype(BF16), oh.astype(BF16))
     parts = [acc[f * slabs : (f + 1) * slabs] for f in range(len(fields))]
-    meta_ref[0] = parts[0]
-    meta_ref[1] = parts[1]
-    meta_ref[2] = parts[2] * LANES + parts[3]
-    meta_ref[3] = parts[4] + parts[5] + parts[6]
+    index = (parts[0] * LANES + parts[1]).astype(jnp.int32)
+    index_ref[...] = jnp.minimum(jnp.maximum(index, 0), limit - 1)
+    target = parts[2] * LANES + parts[3]
+    weight = parts[4] + parts[5] + parts[6]
+    for q in range(subdomains):
+        pack_ref[q, top - 8 : top] = jnp.zeros((8, LANES), F32)
+        pack_ref[q, top : top + QUAD] = target[q * QUAD : (q + 1) * QUAD]
+        pack_ref[q, top + QUAD :] = weight[q * QUAD : (q + 1) * QUAD]
 
 
 class Wet:
-    def __init__(self, subdomains, per, mine, x_ref, meta_ref, pack_ref, got_ref, lhs_ref, acc_ref, sems):
-        self.subdomains, self.per, self.mine, self.x_ref, self.meta_ref = subdomains, per, mine, x_ref, meta_ref
-        self.pack_ref, self.got_ref, self.lhs_ref, self.acc_ref, self.sems = pack_ref, got_ref, lhs_ref, acc_ref, sems
+    def __init__(self, subdomains, used, mine, x_ref, rows_ref, index_ref, pack_ref, got_ref, acc_ref, sems):
+        self.used = used
+        self.subdomains, self.mine, self.x_ref, self.rows_ref = subdomains, mine, x_ref, rows_ref
+        self.index_ref, self.pack_ref, self.got_ref, self.acc_ref, self.sems = index_ref, pack_ref, got_ref, acc_ref, sems
         self.width, self.rows = x_ref.shape
-
-    def gather(self, a, ref, to):
-        width, row = self.width, pl.ds(a, 1)
-        high = jnp.broadcast_to(self.meta_ref[0, row, :].astype(jnp.int32), (width, LANES))
-        low = jnp.broadcast_to(self.meta_ref[1, row, :].astype(jnp.int32), (width, LANES))
-        got = jnp.zeros((width, LANES), F32)
-        for h in range(self.rows // LANES):
-            piece = lane_gather(self.x_ref[:, h * LANES : (h + 1) * LANES], low)
-            got = jnp.where(high == h, piece, got)
-        ref[to, :width, :] = got * self.meta_ref[3, row, :]
-        ref[to, width:, :] = jnp.broadcast_to(self.meta_ref[2, row, :], (META, LANES))
+        self.top = pack_ref.shape[1] - 2 * QUAD
+
+    def prepare(self):
+        lanes = lax.broadcasted_iota(jnp.int32, (LANES, 2 * LANES), 1)
+        subs = lax.broadcasted_iota(jnp.int32, (LANES, 2 * LANES), 0)
+        eyes = jnp.where(lanes % LANES == subs, 1.0, 0.0).astype(BF16)
+
+        def body(t, carry):
+            at = pl.ds(pl.multiple_of(t * LANES, LANES), LANES)
+            hi, lo = split2(self.x_ref[:, at])
+            both = jnp.concatenate([hi, lo], axis=1)
+            self.rows_ref[at, :] = nt(eyes, jnp.concatenate([both] * QUAD, axis=0))
+            return carry
+
+        lax.fori_loop(0, self.rows // LANES, body, 0, unroll=4)
+
+    def gather(self, q):
+        lane = lax.broadcasted_iota(jnp.int32, (1, LANES), 1)
+        masks = [lane < LANES * (g + 1) // QUAD for g in range(QUAD - 1)]
+        for row in range(self.used):
+            line = [self.rows_ref[self.index_ref[q * QUAD + g, row]][None, :] for g in range(QUAD)]
+            got = line[-1]
+            for g in reversed(range(QUAD - 1)):
+                got = jnp.where(masks[g], line[g], got)
+            self.pack_ref[q, row : row + 1, :] = got
 
     def copy(self, to, at):
-        per = self.per
         return remote(
-            self.pack_ref.at[pl.ds(to * per, per)], self.got_ref.at[pl.ds(at * per, per)], self.sems.at[0, to],
+            self.pack_ref.at[to], self.got_ref.at[at], self.sems.at[0, to],
             self.sems.at[1, at], place(self.subdomains + to),
         )
 
     def send(self, first, last):
-        per, mine = self.per, self.mine
-
         def body(s, carry):
-            q = lax.rem(mine + s, self.subdomains)
-
-            def one(p, inner):
-                self.gather(q * per + p, self.pack_ref, q * per + p)
-                return inner
-
-            lax.fori_loop(0, per, one, 0)
-            self.copy(q, mine).start()
+            q = lax.rem(self.mine + s, self.subdomains)
+            self.gather(q)
+
+            @pl.when(s < self.subdomains)
+            def _():
+                self.copy(q, self.mine).start()
+
             return carry
 
         lax.fori_loop(first, last, body, 0)
 
-    def keep(self):
-        def one(p, inner):
-            self.gather(self.mine * self.per + p, self.got_ref, self.mine * self.per + p)
-            return inner
-
-        lax.fori_loop(0, self.per, one, 0)
-
-    def add(self, q):
-        width, wide = self.width, 2 * LANES
+    def add(self, sources, first):
+        width, wide, top = self.width, 2 * LANES, self.top
         highs = self.rows // wide
-        got_ref, lhs_ref = self.got_ref, self.lhs_ref
-        ohs = []
-        for s in range(self.per):
-            a = q * self.per + s
-            target = got_ref[a, width : width + 1, :].astype(jnp.int32)
-            vals = got_ref[a, :width, :]
-            hi = vals.astype(BF16).astype(F32)
-            lo = vals - hi
-            high = jnp.broadcast_to(target // wide, (width, LANES))
-            low = target % wide
-            at = s * wide
-            for h in range(highs):
-                hit = high == h
-                band = slice(h * width, (h + 1) * width)
-                lhs_ref[band, at : at + LANES] = jnp.where(hit, hi, 0.0).astype(BF16)
-                lhs_ref[band, at + LANES : at + wide] = jnp.where(hit, lo, 0.0).astype(BF16)
-            oh = jnp.where(
-                lax.broadcasted_iota(jnp.int32, (wide, LANES), 0) == low, 1.0, 0.0
-            ).astype(BF16)
-            ohs += [oh, oh]
-        self.acc_ref[...] += nt(lhs_ref[...], jnp.concatenate(ohs, axis=1))
-
-    def receive(self):
+        pad = jnp.zeros((LANES - top - 2 * QUAD, LANES), F32)
+        subs = lax.broadcasted_iota(jnp.int32, (wide, LANES), 0).astype(F32).astype(BF16)
+        one, zero = jnp.ones((wide, LANES), BF16), jnp.zeros((wide, LANES), BF16)
+        none = jnp.zeros((width, LANES), BF16)
+        terms, high, ohs = [], [], []
+        for ref, q in sources:
+            turned = jnp.concatenate([ref[q], pad], axis=0).T
+            for g in range(QUAD):
+                target = ref[q, top + g : top + g + 1].astype(jnp.int32)
+                vals = turned[g * width : (g + 1) * width] * ref[q, top + QUAD + g : top + QUAD + g + 1]
+                terms.append(split2(vals))
+                high.append(jnp.broadcast_to((target // wide).astype(F32), (width, LANES)).astype(BF16))
+                low = jnp.broadcast_to((target % wide).astype(F32), (wide, LANES)).astype(BF16)
+                oh = jnp.where(subs == low, one, zero)
+                ohs += [oh, oh]
+        bands = []
+        for h in range(highs):
+            level = jnp.full((width, LANES), h, F32).astype(BF16)
+            bands.append(
+                jnp.concatenate([jnp.where(up == level, t, none) for up, two in zip(high, terms) for t in two], axis=1)
+            )
+        more = nt(jnp.concatenate(bands, axis=0), jnp.concatenate(ohs, axis=1))
+        if first:
+            self.acc_ref[...] = more
+        else:
+            self.acc_ref[...] += more
+
+    def receive(self, first, last):
         subdomains, mine = self.subdomains, self.mine
-        self.acc_ref[...] = jnp.zeros_like(self.acc_ref)
-        self.add(mine)
-
-        def take(s, carry):
+
+        def arrived(s):
             q = lax.rem(mine + subdomains - s, subdomains)
             self.copy(q, q).wait_recv()
-            self.add(q)
+            return self.got_ref, q
+
+        def take(s, carry):
+            self.add([arrived(2 * s), arrived(2 * s + 1)], False)
             return carry
 
-        lax.fori_loop(1, subdomains, take, 0)
+        if first == 0:
+            self.add([(self.pack_ref, mine), arrived(1)], True)
+        lax.fori_loop(max(first, 1), last, take, 0)
 
     def drain(self):
         def body(s, carry):
@@ -215,7 +232,7 @@
         right_ref[to] = both[:, LANES:].reshape(LANES // PART, PART, LANES)
         return carry
 
-    lax.fori_loop(0, x_ref.shape[1] // LANES, body, 0)
+    lax.fori_loop(0, x_ref.shape[1] // LANES, body, 0, unroll=4)
 
 
 def shell_rows(group, cols_ref, blocks_ref, left_ref, right_ref, even_ref, odd_ref):
@@ -226,7 +243,7 @@
     front = lane < LANES // 2
     for r in range(8):
         row = group * 8 + r
-        at = [cols_ref[row, b] * (BS // PART) for b in range(NB)]
+        at = [cols_ref[b, row] * (BS // PART) for b in range(NB)]
         outs = []
         for s in range(3):
             v = jnp.concatenate(
@@ -386,7 +403,7 @@
         self.bulk(self.total, self.total, 4).wait_send()
 
 
-def step_kernel(names, subdomains, per, total_rows, *refs):
+def step_kernel(names, subdomains, used, total_rows, *refs):
     r = dict(zip(names, refs))
     n = 2 * subdomains
     sec, g, d = (lax.axis_index(axis) for axis in ALL)
@@ -411,7 +428,7 @@
         at = pl.ds(pl.multiple_of(i * span, 8), span)
         return pltpu.make_async_copy(r["blocks_hbm"].at[:, at], r["blocks"].at[:, at], r["block_sems"].at[i])
 
-    structure = ("match", "weight")
+    structure = ("match", "weight", "cols")
     fluid = ("src", "dest", "tgt", "w", "diag")
     local("x", 0).start()
 
@@ -431,6 +448,7 @@
             local(name, 1 + i).start()
 
     barrier = announce()
+    index_copy = pltpu.make_async_copy(r["index"], r["index_smem"], r["local_sems"].at[6])
     local("x", 0).wait()
 
     @pl.when(sec == 0)
@@ -441,7 +459,8 @@
     def _():
         for i, name in enumerate(fluid):
             local(name, 1 + i).wait()
-        wet_sort(subdomains, per, r["src"], r["dest"], r["tgt"], r["w"], r["meta"])
+        wet_sort(subdomains, rows, r["src"], r["dest"], r["tgt"], r["w"], r["index"], r["pack"])
+        index_copy.start()
 
     pl.semaphore_wait(barrier, n - 1)
     partners = [
@@ -478,6 +497,30 @@
     def _():
         edge_copy(0).start()
         edge_copy(1).start()
+
+    wet = Wet(
+        subdomains, used, mine, r["xs"], r["wet_rows"], r["index_smem"], r["pack"], r["got"], r["acc"], r["wet_sems"]
+    )
+
+    def shell(first, last):
+        def body(i, carry):
+            block_copy(i).wait()
+            shell_rows(i, r["cols"], r["blocks"], r["left"], r["right"], r["even"], r["odd"])
+            return carry
+
+        lax.fori_loop(first, last, body, 0)
+
+    @pl.when(sec == 0)
+    def _():
+        local("cols", 3).wait()
+        shell(0, groups)
+
+    @pl.when(sec == 1)
+    def _():
+        twin_copy().wait_recv()
+        wet.prepare()
+        index_copy.wait()
+        wet.send(1, subdomains + 1)
 
     def product(i, carry):
         same, mixed = carry
@@ -494,44 +537,22 @@
     cross_sum = Reduce(r["g_stage"], r["g_slots"], r["g_along"], r["g_total"], r["g_sems"])
     cross_sum.stage[...] = part.reshape(cross_sum.stage.shape)
     cross_sum.scatter()
-    wet = Wet(
-        subdomains, per, mine, r["xs"], r["meta"], r["pack"], r["got"], r["lhs"], r["acc"], r["wet_sems"]
-    )
-
-    def shell(first, last):
-        def body(i, carry):
-            block_copy(i).wait()
-            shell_rows(i, r["cols"], r["blocks"], r["left"], r["right"], r["even"], r["odd"])
-            return carry
-
-        lax.fori_loop(first, last, body, 0)
 
     @pl.when(sec == 0)
     def _():
-        shell(0, groups // 2)
+        shell_store(r["even"], r["odd"], image_ref)
+
+    pairs = subdomains // 2
 
     @pl.when(sec == 1)
     def _():
-        twin_copy().wait_recv()
-        wet.send(1, subdomains // 2)
+        wet.receive(0, pairs // 2)
 
     cross_sum.middle()
 
     @pl.when(sec == 0)
     def _():
-        shell(groups // 2, groups)
-
-    @pl.when(sec == 1)
-    def _():
-        wet.send(subdomains // 2, subdomains)
-        wet.keep()
-
-    cross_sum.gather()
-
-    @pl.when(sec == 0)
-    def _():
-        shell_store(r["even"], r["odd"], image_ref)
-        for i, name in enumerate(structure):
+        for i, name in enumerate(structure[:2]):
             local(name, 1 + i).wait()
         for m in range(ROUNDS):
             face_copy(m).wait()
@@ -540,12 +561,13 @@
 
     @pl.when(sec == 1)
     def _():
-        wet.receive()
+        wet.receive(pairs // 2, pairs)
         edge_copy(0).wait()
         edge_copy(1).wait()
         fluid_image(mine, subdomains, x_ref, r["diag"], r["edge"], r["acc"], image_ref)
         wet.drain()
 
+    cross_sum.gather()
     ih, il = split2(image_ref[...])
     both = nt(jnp.concatenate([ih, il], axis=0), high_ref[...])
     head = both[:width] + both[width:] + nt(ih, low_ref[...])
@@ -587,10 +609,10 @@
     eye = jnp.where(sub + width == lane, 1.0, 0.0)
     work = jnp.concatenate([gram, jnp.zeros((width, width), F32)], axis=1) + eye
     for j in range(width):
-        root = jnp.sqrt(work[j : j + 1, j : j + 1])
-        row = work[j : j + 1, :] / root
-        column = work[:, j : j + 1] / root
-        work = jnp.where(sub == j, row, jnp.where(sub > j, work - column * row, work))
+        row = work[j : j + 1, :] / work[j : j + 1, j : j + 1]
+        work = jnp.where(sub > j, work - work[:, j : j + 1] * row, work)
+    pivots = jnp.sum(jnp.where(sub == lane, work, 0.0), axis=1, keepdims=True)
+    work = work / jnp.sqrt(pivots)
     r["fac"][...] = jnp.where(sub <= lane, work, 0.0)[:, :width]
     inverse = work[:, width:]
     mix = -dot(inverse, coef)
@@ -624,8 +646,9 @@
     subdomains = grp * dev
     total_rows = local_rows * lax.axis_size("sec") * subdomains
     capacity = 2 * wet_slots // subdomains + 8
-    per = -(-capacity // LANES)
-    slabs = subdomains * per
+    slabs = subdomains * QUAD
+    used = -(-capacity // QUAD)
+    slots = -(-used // 8) * 8
     flat_prior = prior.reshape(-1, local_rows)
     basis = flat_prior.shape[0]
     plane = 2 * grp
@@ -633,10 +656,10 @@
     tiles = block_values.transpose(1, 0, 2).reshape(NB, group, 8, BS * BS // LANES, LANES)
     tiles = tiles.transpose(0, 1, 3, 2, 4).reshape(NB, row_blocks * BS * BS // LANES, LANES)
     tiled = (wet_slots // LANES, LANES)
-    any_spec, smem = pl.BlockSpec(memory_space=pl.ANY), pl.BlockSpec(memory_space=pltpu.SMEM)
+    any_spec = pl.BlockSpec(memory_space=pl.ANY)
     spec = pl.BlockSpec(memory_space=pltpu.VMEM)
     inputs = {
-        "x_hbm": current, "prior_hbm": flat_prior, "blocks_hbm": tiles, "cols": block_cols,
+        "x_hbm": current, "prior_hbm": flat_prior, "blocks_hbm": tiles, "cols_hbm": block_cols.T,
         "match_hbm": face_match[0], "weight_hbm": face_weight[0], "diag_hbm": fluid_diag[None, :],
         "src_hbm": wet_source.reshape(tiled), "dest_hbm": wet_dest.reshape(tiled),
         "tgt_hbm": wet_target.reshape(tiled), "w_hbm": wet_weight.reshape(tiled),
@@ -647,13 +670,14 @@
         "fac": jax.ShapeDtypeStruct((width, width), F32),
     }
     lanes = -(-(basis + width) // LANES) * LANES
-    slab = pltpu.VMEM((slabs, width + META, LANES), F32)
+    slab = pltpu.VMEM((subdomains, slots + 2 * QUAD, LANES), F32)
     bands = local_rows // (2 * LANES) * width
     field = pltpu.VMEM((width, local_rows), F32)
     cross_piece = pltpu.VMEM((plane, basis // plane, basis), F32)
     head_piece = pltpu.VMEM((plane, width // plane, lanes), F32)
     dma = pltpu.SemaphoreType.DMA
     scratch = {
+        "cols": pltpu.SMEM((NB, row_blocks), jnp.int32),
         "image": field, "x": field, "xs": field,
         "held": pltpu.VMEM((basis, local_rows), F32),
         "high": pltpu.VMEM((basis, local_rows), BF16), "low": pltpu.VMEM((basis, local_rows), BF16),
@@ -667,28 +691,29 @@
         "diag": pltpu.VMEM((1, local_rows), F32),
         "src": pltpu.VMEM(tiled, jnp.int32), "dest": pltpu.VMEM(tiled, jnp.int32),
         "tgt": pltpu.VMEM(tiled, jnp.int32), "w": pltpu.VMEM(tiled, F32),
-        "meta": pltpu.VMEM((4, slabs, LANES), F32),
+        "index": pltpu.VMEM((slabs, LANES), jnp.int32), "index_smem": pltpu.SMEM((slabs, LANES), jnp.int32),
+        "wet_rows": pltpu.VMEM((local_rows, LANES), F32),
         "pack": slab, "got": slab,
-        "lhs": pltpu.VMEM((bands, 2 * per * LANES), BF16), "acc": pltpu.VMEM((bands, 2 * LANES), F32),
+        "acc": pltpu.VMEM((bands, 2 * LANES), F32),
         "g_stage": cross_piece, "g_slots": cross_piece, "g_total": cross_piece,
         "g_along": pltpu.VMEM((dev, basis // plane, basis), F32),
         "h_stage": head_piece, "h_slots": head_piece, "h_total": head_piece,
         "h_along": pltpu.VMEM((dev, width // plane, lanes), F32),
-        "local_sems": dma((6,)), "held_sems": dma((local_rows // 1024,)), "block_sems": dma((group,)),
+        "local_sems": dma((7,)), "held_sems": dma((2,)), "block_sems": dma((group,)),
         "face_sems": dma((2, ROUNDS)), "edge_sems": dma((2, 2)), "twin_sems": dma((2,)),
         "wet_sems": dma((2, subdomains)), "g_sems": dma((6,)), "h_sems": dma((6,)),
     }
     names = (*inputs, *outputs, *scratch)
     next_block, coef, factor = pl.pallas_call(
-        functools.partial(step_kernel, names, subdomains, per, total_rows),
+        functools.partial(step_kernel, names, subdomains, used, total_rows),
         out_shape=tuple(outputs.values()),
-        in_specs=[smem if name == "cols" else any_spec for name in inputs],
+        in_specs=[any_spec] * len(inputs),
         out_specs=(spec,) * len(outputs),
         scratch_shapes=list(scratch.values()),
         compiler_params=pltpu.CompilerParams(
-            vmem_limit_bytes=60 << 20, collective_id=0, has_side_effects=True
+            vmem_limit_bytes=52 << 20, collective_id=0, has_side_effects=True
         ),
-    )(*inputs.values())
+    )(*(pltpu.with_memory_space_constraint(value, pltpu.HBM) for value in inputs.values()))
     return (next_block, coef.reshape(prior.shape[0], width, width), factor)
 
 

time: 72.6 us -> 51.5 us (0.71)
  Pallas kernels: 65.3 us -> 48.6 us
  local copies, waits for them, and re-layouts: 6.34 us -> 2.14 us
    pallas_call x1, Pallas kernels: 65.3 us -> 48.6 us  [shards(): pl.pallas_call(functools.partial(step_kernel, names, subdomains, used, to...]
    unnamed x4 -> x3, local copies, waits for them, and re-layouts: 6.34 us -> 2.14 us
where the time goes in v2:
time: 51.5 us; the launch traced here: 51.3 us
  Pallas kernels  48.6 us (94%)
  local copies, waits for them, and re-layouts  2.14 us (4%)
  between operations  0.64 us (1%)
    pallas_call x1, Pallas kernels, shards(): pl.pallas_call(functools.partial(step_kernel, names, subdomains, used, to...  48.6 us
    unnamed x3, local copies, waits for them, and re-layouts  2.14 us

profile of v2, /device:TPU:0, one launch (start us, length us, event | category | flops | bytes accessed | tf_op | source)
XLA Modules:
  0.0 51.3 jit_solution(4639730482659984542)
XLA Ops:
  0.6 48.6 %shard_map.130 = (f32[32,6144]{1,0:T(8,128)S(1)}, f32[256,32]{1,0:T(8,128)S(1)}, f32[32,32]{1,0:T(8,128)S(1)}) custom-call(f32[32,6144]{1,0:T(8,128)} %refs_0_.1, f32[256,6144]{1,0:T(8,128)} %bitcast.19, f32[6,4608,128]{2,1,0:T(8,128)} %bitcast.18, s32[6,64]{1,0:T(8,128)} %bitcast.27, s32[4,1536]{1,0:T(4,128)} %bitcast.20, f32[4,1536]{1,0:T(4,128)} %bitcast.21, ...), custom_call_target="tpu_custom_call" | custom-call | tf_op jit(solution)/shard_map/pallas_call | solution.py:707
  49.2 0.9 %copy.17 = f32[32,6144]{1,0:T(8,128)} copy(f32[32,6144]{1,0:T(8,128)S(1)} %get-tuple-element.12) | data formatting | bytes 1572864
  50.1 0.7 %copy.18 = f32[8,32,32]{2,1,0:T(8,128)} copy(f32[8,32,32]{2,1,0:T(8,128)S(1)} %bitcast.17) | data formatting | bytes 65536
  50.7 0.6 %copy.19 = f32[32,32]{1,0:T(8,128)} copy(f32[32,32]{1,0:T(8,128)S(1)} %get-tuple-element.14) | data formatting | bytes 8192

commit v3 on v2

--- a/solution.py
+++ b/solution.py
@@ -76,46 +76,48 @@
         acc = acc + nt(lhs.astype(BF16), oh.astype(BF16))
     parts = [acc[f * slabs : (f + 1) * slabs] for f in range(len(fields))]
     index = (parts[0] * LANES + parts[1]).astype(jnp.int32)
-    index_ref[...] = jnp.minimum(jnp.maximum(index, 0), limit - 1)
+    index = jnp.minimum(jnp.maximum(index, 0), limit - 1)
     target = parts[2] * LANES + parts[3]
     weight = parts[4] + parts[5] + parts[6]
     for q in range(subdomains):
+        index_ref[q] = index[q * QUAD : (q + 1) * QUAD]
         pack_ref[q, top - 8 : top] = jnp.zeros((8, LANES), F32)
         pack_ref[q, top : top + QUAD] = target[q * QUAD : (q + 1) * QUAD]
         pack_ref[q, top + QUAD :] = weight[q * QUAD : (q + 1) * QUAD]
 
 
 class Wet:
-    def __init__(self, subdomains, used, mine, x_ref, rows_ref, index_ref, pack_ref, got_ref, acc_ref, sems):
-        self.used = used
+    def __init__(
+        self, subdomains, used, mine, x_ref, rows_ref, index_ref, index_smem, index_sems, pack_ref, got_ref,
+        acc_ref, sems,
+    ):
+        self.used, self.index_smem, self.index_sems = used, index_smem, index_sems
         self.subdomains, self.mine, self.x_ref, self.rows_ref = subdomains, mine, x_ref, rows_ref
         self.index_ref, self.pack_ref, self.got_ref, self.acc_ref, self.sems = index_ref, pack_ref, got_ref, acc_ref, sems
         self.width, self.rows = x_ref.shape
         self.top = pack_ref.shape[1] - 2 * QUAD
 
-    def prepare(self):
-        lanes = lax.broadcasted_iota(jnp.int32, (LANES, 2 * LANES), 1)
-        subs = lax.broadcasted_iota(jnp.int32, (LANES, 2 * LANES), 0)
-        eyes = jnp.where(lanes % LANES == subs, 1.0, 0.0).astype(BF16)
-
+    def prepare(self, first, last):
         def body(t, carry):
             at = pl.ds(pl.multiple_of(t * LANES, LANES), LANES)
-            hi, lo = split2(self.x_ref[:, at])
-            both = jnp.concatenate([hi, lo], axis=1)
-            self.rows_ref[at, :] = nt(eyes, jnp.concatenate([both] * QUAD, axis=0))
+            self.rows_ref[at, :] = jnp.concatenate([self.x_ref[:, at]] * QUAD, axis=0).T
             return carry
 
-        lax.fori_loop(0, self.rows // LANES, body, 0, unroll=4)
-
-    def gather(self, q):
+        lax.fori_loop(first, last, body, 0, unroll=4)
+
+    def gather(self, b, q):
         lane = lax.broadcasted_iota(jnp.int32, (1, LANES), 1)
         masks = [lane < LANES * (g + 1) // QUAD for g in range(QUAD - 1)]
         for row in range(self.used):
-            line = [self.rows_ref[self.index_ref[q * QUAD + g, row]][None, :] for g in range(QUAD)]
+            line = [self.rows_ref[self.index_smem[b, g, row]][None, :] for g in range(QUAD)]
             got = line[-1]
             for g in reversed(range(QUAD - 1)):
                 got = jnp.where(masks[g], line[g], got)
             self.pack_ref[q, row : row + 1, :] = got
+
+    def index_copy(self, b, s):
+        q = lax.rem(self.mine + s, self.subdomains)
+        return pltpu.make_async_copy(self.index_ref.at[q], self.index_smem.at[b], self.index_sems.at[b])
 
     def copy(self, to, at):
         return remote(
@@ -123,18 +125,24 @@
             self.sems.at[1, at], place(self.subdomains + to),
         )
 
-    def send(self, first, last):
-        def body(s, carry):
-            q = lax.rem(self.mine + s, self.subdomains)
-            self.gather(q)
-
-            @pl.when(s < self.subdomains)
-            def _():
-                self.copy(q, self.mine).start()
+    def send(self):
+        def body(t, carry):
+            for b in range(2):
+                s = 2 * t + 1 + b
+                q = lax.rem(self.mine + s, self.subdomains)
+                self.index_copy(b, s).wait()
+                self.gather(b, q)
+                self.index_copy(b, s + 2).start()
+
+                @pl.when(s < self.subdomains)
+                def _():
+                    self.copy(q, self.mine).start()
 
             return carry
 
-        lax.fori_loop(first, last, body, 0)
+        lax.fori_loop(0, self.subdomains // 2, body, 0)
+        for b in range(2):
+            self.index_copy(b, self.subdomains + 1 + b).wait()
 
     def add(self, sources, first):
         width, wide, top = self.width, 2 * LANES, self.top
@@ -424,7 +432,7 @@
         return pltpu.make_async_copy(r["prior_hbm"].at[:, at], held.at[:, at], r["held_sems"].at[i])
 
     def block_copy(i):
-        span = r["blocks"].shape[1] // groups
+        span = r["blocks_hbm"].shape[1] // groups
         at = pl.ds(pl.multiple_of(i * span, 8), span)
         return pltpu.make_async_copy(r["blocks_hbm"].at[:, at], r["blocks"].at[:, at], r["block_sems"].at[i])
 
@@ -448,7 +456,9 @@
             local(name, 1 + i).start()
 
     barrier = announce()
-    index_copy = pltpu.make_async_copy(r["index"], r["index_smem"], r["local_sems"].at[6])
+    wet = Wet(
+        subdomains, used, mine, r["xs"], r["wet_rows"], r["index"], r["index_smem"], r["index_sems"], r["pack"], r["got"], r["acc"], r["wet_sems"]
+    )
     local("x", 0).wait()
 
     @pl.when(sec == 0)
@@ -460,7 +470,8 @@
         for i, name in enumerate(fluid):
             local(name, 1 + i).wait()
         wet_sort(subdomains, rows, r["src"], r["dest"], r["tgt"], r["w"], r["index"], r["pack"])
-        index_copy.start()
+        for b in range(2):
+            wet.index_copy(b, 1 + b).start()
 
     pl.semaphore_wait(barrier, n - 1)
     partners = [
@@ -484,12 +495,16 @@
             r["edge_sems"].at[1, side], place(to),
         )
 
-    def twin_copy():
-        return remote(x_ref, r["xs"], r["twin_sems"].at[0], r["twin_sems"].at[1], (1, g, d))
+    def twin_copy(m):
+        at = pl.ds(m * face, face)
+        return remote(
+            x_ref.at[:, at], r["xs"].at[:, at], r["twin_sems"].at[0, m], r["twin_sems"].at[1, m], (1, g, d)
+        )
 
     @pl.when(sec == 0)
     def _():
-        twin_copy().start()
+        for m in range(ROUNDS):
+            twin_copy(m).start()
         for m in range(ROUNDS):
             face_copy(m).start()
 
@@ -498,9 +513,6 @@
         edge_copy(0).start()
         edge_copy(1).start()
 
-    wet = Wet(
-        subdomains, used, mine, r["xs"], r["wet_rows"], r["index_smem"], r["pack"], r["got"], r["acc"], r["wet_sems"]
-    )
 
     def shell(first, last):
         def body(i, carry):
@@ -517,10 +529,10 @@
 
     @pl.when(sec == 1)
     def _():
-        twin_copy().wait_recv()
-        wet.prepare()
-        index_copy.wait()
-        wet.send(1, subdomains + 1)
+        for m in range(ROUNDS):
+            twin_copy(m).wait_recv()
+            wet.prepare(m * face // LANES, (m + 1) * face // LANES)
+        wet.send()
 
     def product(i, carry):
         same, mixed = carry
@@ -535,6 +547,8 @@
     same, mixed = lax.fori_loop(0, rows // chunk, product, (zero, zero))
     part = same + mixed + mixed.T
     cross_sum = Reduce(r["g_stage"], r["g_slots"], r["g_along"], r["g_total"], r["g_sems"])
+    half = basis // 2
+    part = jnp.concatenate([part[:half, :half], part[:half, half:], part[half:, half:]], axis=0)
     cross_sum.stage[...] = part.reshape(cross_sum.stage.shape)
     cross_sum.scatter()
 
@@ -557,7 +571,8 @@
         for m in range(ROUNDS):
             face_copy(m).wait()
         add_faces(r["faces"], r["match"], r["weight"], image_ref)
-        twin_copy().wait_send()
+        for m in range(ROUNDS):
+            twin_copy(m).wait_send()
 
     @pl.when(sec == 1)
     def _():
@@ -584,25 +599,39 @@
     cross_sum.finish()
     cross_sum.drain()
     head_sum.middle()
+    blocks = cross_sum.total[...].reshape(3 * half, half)
+    corner = blocks[half : 2 * half]
+    cross = jnp.concatenate(
+        [
+            jnp.concatenate([blocks[:half], corner], axis=1),
+            jnp.concatenate([corner.T, blocks[2 * half :]], axis=1),
+        ],
+        axis=0,
+    )
+    highest = lax.Precision.HIGHEST
+
+    def dot(a, b):
+        return jnp.dot(a, b, precision=highest, preferred_element_type=F32)
+
+    def dot_nt(a, b):
+        return lax.dot_general(a, b, NT, precision=highest, preferred_element_type=F32)
+
+    eye = jnp.where(
+        lax.broadcasted_iota(jnp.int32, (basis, basis), 0) == lax.broadcasted_iota(jnp.int32, (basis, basis), 1),
+        1.0,
+        0.0,
+    )
+    twice = 2.0 * eye - cross
+    r["twice"][...] = twice
+    r["drop"][...] = 2.0 * twice - dot(twice, dot(cross, twice))
     head_sum.gather()
     head_sum.finish()
     head_sum.drain()
-    cross = cross_sum.total[...].reshape(basis, basis)
     summed = jnp.concatenate([head_sum.total[i] for i in range(count)], axis=0)
     first = summed[:, :basis]
     square = summed[:, basis : basis + width]
-    highest = lax.Precision.HIGHEST
-
-    def dot(a, b):
-        return jnp.dot(a, b, precision=highest, preferred_element_type=F32)
-
-    def dot_nt(a, b):
-        return lax.dot_general(a, b, NT, precision=highest, preferred_element_type=F32)
-
-    coef = 2.0 * first - dot(first, cross)
-    gram = (
-        square - dot_nt(coef, first) - dot_nt(first, coef) + dot_nt(dot(coef, cross), coef)
-    ) * (1.0 / total_rows)
+    coef = dot(first, r["twice"][...])
+    gram = (square - dot_nt(dot(first, r["drop"][...]), first)) * (1.0 / total_rows)
     r["coef"][...] = coef.T
     sub = lax.broadcasted_iota(jnp.int32, (width, 2 * width), 0)
     lane = lax.broadcasted_iota(jnp.int32, (width, 2 * width), 1)
@@ -632,6 +661,15 @@
         return carry
 
     lax.fori_loop(0, rows // chunk, out, 0)
+
+
+def settle_kernel(*refs):
+    count = (len(refs) - 1) // 2
+    copies = [pltpu.make_async_copy(refs[i], refs[count + i], refs[-1].at[i]) for i in range(count)]
+    for copy in copies:
+        copy.start()
+    for copy in copies:
+        copy.wait()
 
 
 def shards(
@@ -673,7 +711,7 @@
     slab = pltpu.VMEM((subdomains, slots + 2 * QUAD, LANES), F32)
     bands = local_rows // (2 * LANES) * width
     field = pltpu.VMEM((width, local_rows), F32)
-    cross_piece = pltpu.VMEM((plane, basis // plane, basis), F32)
+    cross_piece = pltpu.VMEM((plane, 3 * basis // 2 // plane, basis // 2), F32)
     head_piece = pltpu.VMEM((plane, width // plane, lanes), F32)
     dma = pltpu.SemaphoreType.DMA
     scratch = {
@@ -681,7 +719,7 @@
         "image": field, "x": field, "xs": field,
         "held": pltpu.VMEM((basis, local_rows), F32),
         "high": pltpu.VMEM((basis, local_rows), BF16), "low": pltpu.VMEM((basis, local_rows), BF16),
-        "blocks": pltpu.VMEM(tiles.shape, F32),
+        "blocks": pltpu.VMEM((NB, tiles.shape[1] + 32, LANES), F32),
         "left": pltpu.VMEM((local_rows // PART, PART, LANES), BF16),
         "right": pltpu.VMEM((local_rows // PART, PART, LANES), BF16),
         "even": pltpu.VMEM((local_rows // 4, LANES), F32), "odd": pltpu.VMEM((local_rows // 4, LANES), F32),
@@ -691,16 +729,18 @@
         "diag": pltpu.VMEM((1, local_rows), F32),
         "src": pltpu.VMEM(tiled, jnp.int32), "dest": pltpu.VMEM(tiled, jnp.int32),
         "tgt": pltpu.VMEM(tiled, jnp.int32), "w": pltpu.VMEM(tiled, F32),
-        "index": pltpu.VMEM((slabs, LANES), jnp.int32), "index_smem": pltpu.SMEM((slabs, LANES), jnp.int32),
+        "index": pltpu.VMEM((subdomains, QUAD, LANES), jnp.int32),
+        "index_smem": pltpu.SMEM((2, QUAD, LANES), jnp.int32), "index_sems": dma((2,)),
         "wet_rows": pltpu.VMEM((local_rows, LANES), F32),
         "pack": slab, "got": slab,
         "acc": pltpu.VMEM((bands, 2 * LANES), F32),
         "g_stage": cross_piece, "g_slots": cross_piece, "g_total": cross_piece,
-        "g_along": pltpu.VMEM((dev, basis // plane, basis), F32),
+        "g_along": pltpu.VMEM((dev, 3 * basis // 2 // plane, basis // 2), F32),
+        "twice": pltpu.VMEM((basis, basis), F32), "drop": pltpu.VMEM((basis, basis), F32),
         "h_stage": head_piece, "h_slots": head_piece, "h_total": head_piece,
         "h_along": pltpu.VMEM((dev, width // plane, lanes), F32),
-        "local_sems": dma((7,)), "held_sems": dma((2,)), "block_sems": dma((group,)),
-        "face_sems": dma((2, ROUNDS)), "edge_sems": dma((2, 2)), "twin_sems": dma((2,)),
+        "local_sems": dma((6,)), "held_sems": dma((2,)), "block_sems": dma((group,)),
+        "face_sems": dma((2, ROUNDS)), "edge_sems": dma((2, 2)), "twin_sems": dma((2, ROUNDS)),
         "wet_sems": dma((2, subdomains)), "g_sems": dma((6,)), "h_sems": dma((6,)),
     }
     names = (*inputs, *outputs, *scratch)
@@ -714,6 +754,14 @@
             vmem_limit_bytes=52 << 20, collective_id=0, has_side_effects=True
         ),
     )(*(pltpu.with_memory_space_constraint(value, pltpu.HBM) for value in inputs.values()))
+    next_block, coef, factor = pl.pallas_call(
+        settle_kernel,
+        out_shape=tuple(outputs.values()),
+        in_specs=[spec] * len(outputs),
+        out_specs=(any_spec,) * len(outputs),
+        scratch_shapes=[dma((len(outputs),))],
+        compiler_params=pltpu.CompilerParams(vmem_limit_bytes=8 << 20),
+    )(next_block, coef, factor)
     return (next_block, coef.reshape(prior.shape[0], width, width), factor)
 
 

time: 51.5 us -> 49.6 us (0.963)
  local copies, waits for them, and re-layouts: 2.14 us -> 0 us
    unnamed x3 -> x0, local copies, waits for them, and re-layouts: 2.14 us -> none
    pallas_call x0 -> x1, Pallas kernels: none -> 0.94 us  [shards(): pl.pallas_call(settle_kernel, out_shape=tuple(outputs.values()), in_specs...]
    pallas_call x1, Pallas kernels: 48.6 us -> 47.7 us  [shards(): pl.pallas_call(functools.partial(step_kernel, names, subdomains, used, to...]
where the time goes in v3:
time: 49.6 us; the launch traced here: 49.4 us
  Pallas kernels  48.6 us (98%)
  between operations  0.8 us (2%)
    pallas_call x1, Pallas kernels, shards(): pl.pallas_call(functools.partial(step_kernel, names, subdomains, used, to...  47.7 us

profile of v3, /device:TPU:0, one launch (start us, length us, event | category | flops | bytes accessed | tf_op | source)
XLA Modules:
  0.0 49.4 jit_solution(965646776771578986)
XLA Ops:
  0.6 47.7 %shard_map.130 = (f32[32,6144]{1,0:T(8,128)S(1)}, f32[256,32]{1,0:T(8,128)S(1)}, f32[32,32]{1,0:T(8,128)S(1)}) custom-call(f32[32,6144]{1,0:T(8,128)} %refs_0_.1, f32[256,6144]{1,0:T(8,128)} %bitcast.18, f32[6,4608,128]{2,1,0:T(8,128)} %bitcast.17, s32[6,64]{1,0:T(8,128)} %bitcast.26, s32[4,1536]{1,0:T(4,128)} %bitcast.19, f32[4,1536]{1,0:T(4,128)} %bitcast.20, ...), custom_call_target="tpu_custom_call" | custom-call | tf_op jit(solution)/shard_map/pallas_call | solution.py:747
  48.3 0.9 %shard_map.131 = (f32[32,6144]{1,0:T(8,128)}, f32[256,32]{1,0:T(8,128)}, f32[32,32]{1,0:T(8,128)}) custom-call(f32[32,6144]{1,0:T(8,128)S(1)} %get-tuple-element.9.refs_0_, f32[256,32]{1,0:T(8,128)S(1)} %get-tuple-element.10.refs_1_, f32[32,32]{1,0:T(8,128)S(1)} %get-tuple-element.11.refs_2_), custom_call_target="tpu_custom_call" | custom-call | tf_op jit(solution)/shard_map/pallas_call | solution.py:757

commit v4 on v3

--- a/solution.py
+++ b/solution.py
@@ -522,8 +522,29 @@
 
         lax.fori_loop(first, last, body, 0)
 
+    half = basis // 2
+    cross_sum = Reduce(r["g_stage"], r["g_slots"], r["g_along"], r["g_total"], r["g_sems"])
+
+    def cross_part():
+        def product(i, carry):
+            same, mixed = carry
+            prior_copy(i).wait()
+            at = pl.ds(pl.multiple_of(i * chunk, chunk), chunk)
+            hi, lo = split2(held[:, at])
+            high_ref[:, at] = hi
+            low_ref[:, at] = lo
+            return same + nt(hi, hi), mixed + nt(hi, lo)
+
+        zero = jnp.zeros((basis, basis), F32)
+        same, mixed = lax.fori_loop(0, rows // chunk, product, (zero, zero))
+        part = same + mixed + mixed.T
+        part = jnp.concatenate([part[:half, :half], part[:half, half:], part[half:, half:]], axis=0)
+        cross_sum.stage[...] = part.reshape(cross_sum.stage.shape)
+        cross_sum.scatter()
+
     @pl.when(sec == 0)
     def _():
+        cross_part()
         local("cols", 3).wait()
         shell(0, groups)
 
@@ -533,24 +554,8 @@
             twin_copy(m).wait_recv()
             wet.prepare(m * face // LANES, (m + 1) * face // LANES)
         wet.send()
-
-    def product(i, carry):
-        same, mixed = carry
-        prior_copy(i).wait()
-        at = pl.ds(pl.multiple_of(i * chunk, chunk), chunk)
-        hi, lo = split2(held[:, at])
-        high_ref[:, at] = hi
-        low_ref[:, at] = lo
-        return same + nt(hi, hi), mixed + nt(hi, lo)
-
-    zero = jnp.zeros((basis, basis), F32)
-    same, mixed = lax.fori_loop(0, rows // chunk, product, (zero, zero))
-    part = same + mixed + mixed.T
-    cross_sum = Reduce(r["g_stage"], r["g_slots"], r["g_along"], r["g_total"], r["g_sems"])
-    half = basis // 2
-    part = jnp.concatenate([part[:half, :half], part[:half, half:], part[half:, half:]], axis=0)
-    cross_sum.stage[...] = part.reshape(cross_sum.stage.shape)
-    cross_sum.scatter()
+        cross_part()
+
 
     @pl.when(sec == 0)
     def _():
@@ -577,12 +582,15 @@
     @pl.when(sec == 1)
     def _():
         wet.receive(pairs // 2, pairs)
+    cross_sum.gather()
+
+    @pl.when(sec == 1)
+    def _():
         edge_copy(0).wait()
         edge_copy(1).wait()
         fluid_image(mine, subdomains, x_ref, r["diag"], r["edge"], r["acc"], image_ref)
         wet.drain()
 
-    cross_sum.gather()
     ih, il = split2(image_ref[...])
     both = nt(jnp.concatenate([ih, il], axis=0), high_ref[...])
     head = both[:width] + both[width:] + nt(ih, low_ref[...])

time: 49.6 us -> 49.5 us (level)
  no operation moved by 1% of the time
where the time goes in v4:
time: 49.5 us; the launch traced here: 49.4 us
  Pallas kernels  48.6 us (98%)
  between operations  0.8 us (2%)
    pallas_call x1, Pallas kernels, shards(): pl.pallas_call(functools.partial(step_kernel, names, subdomains, used, to...  47.7 us

profile of v4, /device:TPU:0, one launch (start us, length us, event | category | flops | bytes accessed | tf_op | source)
XLA Modules:
  0.0 49.4 jit_solution(11418442480672976305)
XLA Ops:
  0.6 47.7 %shard_map.130 = (f32[32,6144]{1,0:T(8,128)S(1)}, f32[256,32]{1,0:T(8,128)S(1)}, f32[32,32]{1,0:T(8,128)S(1)}) custom-call(f32[32,6144]{1,0:T(8,128)} %refs_0_.1, f32[256,6144]{1,0:T(8,128)} %bitcast.18, f32[6,4608,128]{2,1,0:T(8,128)} %bitcast.17, s32[6,64]{1,0:T(8,128)} %bitcast.26, s32[4,1536]{1,0:T(4,128)} %bitcast.19, f32[4,1536]{1,0:T(4,128)} %bitcast.20, ...), custom_call_target="tpu_custom_call" | custom-call | tf_op jit(solution)/shard_map/pallas_call | solution.py:755
  48.3 0.9 %shard_map.131 = (f32[32,6144]{1,0:T(8,128)}, f32[256,32]{1,0:T(8,128)}, f32[32,32]{1,0:T(8,128)}) custom-call(f32[32,6144]{1,0:T(8,128)S(1)} %get-tuple-element.9.refs_0_, f32[256,32]{1,0:T(8,128)S(1)} %get-tuple-element.10.refs_1_, f32[32,32]{1,0:T(8,128)S(1)} %get-tuple-element.11.refs_2_), custom_call_target="tpu_custom_call" | custom-call | tf_op jit(solution)/shard_map/pallas_call | solution.py:765
